TPU v7x, 256 devices: a whole 4x4x8 slice. The times are simulated.
256 devices in a mesh: row: 16 (over z_lo, y, core), col: 16 (over z_hi, x).
Axes of the slice: x: 4, y: 4, z: 8 (z_hi: 4, z_lo: 2; z = z_hi * 2 + z_lo), core: 2. Of those that a mesh axis runs over, the one named last changes fastest.
Arguments:
- page_scores: bfloat16 [393216, 128], P('row'), may hold values from -6 to 6
- tile_values: bfloat16 [16, 16, 22, 512, 512], P('row', 'col'), may hold values from -0.25 to 0.25
- tile_row: int32 [16, 16, 22], P('row', 'col'), may hold values from 0 to 47, as said below
- tile_col: int32 [16, 16, 22], P('row', 'col'), may hold values from 0 to 7, as said below
- tile_count: int32 [16, 16], P('row', 'col'), may hold values from 2 to 22, as said below
- page_seed: int32 [393216], P(('row', 'col')), may hold values 0 or 1
- page_label: int32 [393216], P(('row', 'col')), may hold values from 0 to 127
- page_degree: int32 [393216], P(('row', 'col')), may hold values from 4 to 64
- feature_seed: int32 [65536], P('col'), may hold values 0 or 1
- feature_label: int32 [65536], P('col'), may hold values from 0 to 127
- feature_degree: int32 [65536], P('col'), may hold values from 4 to 64
Outputs:
- new_page_scores: bfloat16 [393216, 128], P(('row', 'col'))
Inputs may be any that keep to these rules, and one draw needn't show every extreme that they name: `tile_row`: within each grid cell the first tile_count slots name distinct tile positions; later slots are unused. `tile_col`: paired with tile_row slot by slot. `tile_count`: some grid cell has all 22 slots live in every draw.
All inputs are finite; a program needn't handle non-finite values. No bound on the sum of `page_seed` or of `feature_seed` on one device may be relied on, other than what follows from the above.
Results may differ from a plain program's by a relative error of at most 0.0047.
Values may be sent and summed in bfloat16 or wider, within the bound.
No kernel may reach another device: no remote copies, remote signals or barrier semaphores. Data moves between devices by JAX's collectives and lax.ppermute only.
A program may use at most 128 MiB of HBM per device.

v0:
```python
import functools

import jax
import jax.numpy as jnp
from jax import lax
from jax.experimental import pallas as pl
from jax.experimental.pallas import tpu as pltpu
from jax.sharding import Mesh, PartitionSpec as P

BF16 = jnp.bfloat16
F32 = jnp.float32
ROW = ("zlo", "y", "core")
CHIPS = ("zlo", "y")
COL = ("zhi", "x")
TILE_DOT = (((1,), (0,)), ((), ()))
TILE_T_DOT = (((0,), (0,)), ((), ()))
SMEM = pl.BlockSpec(memory_space=pltpu.SMEM)
HBM = pl.BlockSpec(memory_space=pl.ANY)
VMEM = pl.BlockSpec(memory_space=pltpu.VMEM)


def clamp(sums, degree, known, label):
    classes = lax.broadcasted_iota(jnp.int32, sums.shape, 1)
    hot = (label[:, None] == classes).astype(F32)
    scaled = sums * lax.rsqrt(degree.astype(F32))[:, None]
    return jnp.where(known[:, None] == 1, hot, scaled).astype(BF16)


def add(*terms):
    total = terms[0].astype(F32)
    for term in terms[1:]:
        total = total + term.astype(F32)
    return total


def feature_kernel(
    row_ref, col_ref, count_ref, place, tiles, pages, own, other, tile_buf, page_buf, acc, sems
):
    edge = tile_buf.shape[1]
    half = edge // 2
    count = count_ref[0]
    core = place[2]

    def copies(slot):
        src = pl.multiple_of(row_ref[slot] * edge, edge)
        return (
            pltpu.make_async_copy(tiles.at[slot], tile_buf.at[slot], sems.at[0, slot]),
            pltpu.make_async_copy(pages.at[pl.ds(src, edge)], page_buf.at[slot], sems.at[1, slot]),
        )

    @pl.loop(0, count)
    def _(slot):
        for copy in copies(slot):
            copy.start()

    acc[...] = jnp.zeros_like(acc)

    @pl.loop(0, count)
    def _(slot):
        for copy in copies(slot):
            copy.wait()
        acc[col_ref[slot]] += lax.dot_general(
            page_buf[slot], tile_buf[slot], TILE_T_DOT, preferred_element_type=F32
        )

    for low, high, here in ((own, other, 0), (other, own, 1)):

        @pl.when(core == here)
        def _():
            @pl.loop(0, acc.shape[0])
            def _(tile):
                low[tile] = acc[tile, :, :half].T
                high[tile] = acc[tile, :, half:].T


def feature_partials(rows, cols, count, place, tiles, pages, feats):
    slots, edge, _ = tiles.shape
    classes = pages.shape[1]
    halves = jax.ShapeDtypeStruct((feats // edge, edge // 2, classes), F32)
    return pl.pallas_call(
        feature_kernel,
        out_shape=[halves, halves],
        in_specs=[SMEM] * 4 + [HBM] * 2,
        out_specs=[VMEM] * 2,
        scratch_shapes=[
            pltpu.VMEM((slots, edge, edge), BF16),
            pltpu.VMEM((slots, edge, classes), BF16),
            pltpu.VMEM((feats // edge, classes, edge), F32),
            pltpu.SemaphoreType.DMA((2, slots)),
        ],
        compiler_params=pltpu.CompilerParams(vmem_limit_bytes=50 << 20),
        cost_estimate=pl.CostEstimate(
            flops=2 * slots * edge * edge * classes,
            bytes_accessed=2 * slots * edge * (edge + classes),
            transcendentals=0,
        ),
        name="feature_partials",
    )(rows, cols, count, place, tiles, pages)


def page_kernel(deltas, straight, per, row_ref, col_ref, count_ref, place, tiles, mine, partner, *rest):
    n_out = 2 * len(deltas)
    outs, rest = rest[:n_out], rest[n_out:]
    if straight:
        first_out, rest = rest[0], rest[1:]
    tile_buf, feats, acc, head, nxt, sems, feat_sems = rest
    edge = tile_buf.shape[1]
    half = edge // 2
    span = 4 * per
    page_tiles = head.shape[0]
    count = count_ref[0]
    core = place[2]

    def feature_copies():
        for which, source in ((core, mine), (1 - core, partner)):
            part = pl.ds(pl.multiple_of(which * half, half), half)
            yield pltpu.make_async_copy(source, feats.at[:, part], feat_sems.at[which])

    for copy in feature_copies():
        copy.start()

    @pl.loop(0, page_tiles, unroll=8)
    def _(r):
        head[r] = -1

    def tile_copy(slot):
        return pltpu.make_async_copy(tiles.at[slot], tile_buf.at[slot], sems.at[slot])

    @pl.loop(0, count)
    def _(slot):
        r = row_ref[slot]
        owner, k = r // per, lax.rem(r, per)
        ahead = lax.rem(lax.rem(owner, 4) - place[0] + 4, 4)
        r = ahead * span + lax.rem(owner // 4 - place[1] + 4, 4) * per + k
        wanted = functools.reduce(jnp.logical_or, [ahead == d for d in deltas])
        if straight:
            wanted = jnp.logical_or(wanted, k == 0)

        @pl.when(wanted)
        def _():
            tile_copy(slot).start()
            nxt[slot] = head[r]
            head[r] = slot

    for out in outs:
        out[...] = jnp.zeros_like(out)
    if straight:
        first_out[...] = jnp.zeros_like(first_out)

    for copy in feature_copies():
        copy.wait()

    def product(slot):
        tile_copy(slot).wait()
        return lax.dot_general(
            tile_buf[slot], feats[col_ref[slot]], TILE_DOT, preferred_element_type=F32
        )

    def visit(delta, index, j):
        first = head[delta * span + index]
        second, k = index // per, lax.rem(index, per)

        @pl.when(first >= 0)
        def _():
            acc[...] = product(first)

            def body(slot):
                acc[...] += product(slot)
                return nxt[slot]

            lax.while_loop(lambda s: s >= 0, body, nxt[first])
            if straight:

                @pl.when(k == 0)
                def _():
                    slow = lax.rem(place[1] + second, 4)
                    fast = lax.rem(place[0] + delta, 4)
                    first_out[slow, fast] = acc[:half, :].astype(BF16)

            for i in range(len(deltas)):

                @pl.when(jnp.logical_and(j == i, k == 0))
                def _():
                    outs[2 * i][second, 0] = acc[half:, :].astype(BF16)

                @pl.when(jnp.logical_and(j == i, k > 0))
                def _():
                    outs[2 * i][second, k] = acc[:half, :].astype(BF16)
                    outs[2 * i + 1][second, k - 1] = acc[half:, :].astype(BF16)

    others = [d for d in range(4) if d not in deltas] if straight else []
    walk = [(d, j, 1) for j, d in enumerate(deltas)] + [(d, -1, per) for d in others]

    @pl.loop(0, len(walk))
    def _(w):
        delta, j, step = [
            functools.reduce(
                lambda v, n: jnp.where(w == n, walk[n][f], v), range(1, len(walk)), jnp.int32(walk[0][f])
            )
            for f in range(3)
        ]

        @pl.loop(0, span // step)
        def _(i):
            visit(delta, i * step, j)


def page_partials(deltas, straight, rows, cols, count, place, tiles, mine, partner, page_tiles):
    slots, edge, _ = tiles.shape
    classes = mine.shape[-1]
    per = page_tiles // 16
    half = edge // 2
    shapes = [(4, per, half, classes), (4, per - 1, half, classes)] * len(deltas)
    if straight:
        shapes.append((4, 4, half, classes))
    share = len(deltas) + (1 if straight else 0)
    out = pl.pallas_call(
        functools.partial(page_kernel, deltas, straight, per),
        out_shape=[jax.ShapeDtypeStruct(s, BF16) for s in shapes],
        in_specs=[SMEM] * 4 + [HBM] * 3,
        out_specs=[VMEM] * len(shapes),
        scratch_shapes=[
            pltpu.VMEM((slots, edge, edge), BF16),
            pltpu.VMEM((mine.shape[0], edge, classes), BF16),
            pltpu.VMEM((edge, classes), F32),
            pltpu.SMEM((page_tiles,), jnp.int32),
            pltpu.SMEM((slots,), jnp.int32),
            pltpu.SemaphoreType.DMA((slots,)),
            pltpu.SemaphoreType.DMA((2,)),
        ],
        compiler_params=pltpu.CompilerParams(vmem_limit_bytes=50 << 20),
        cost_estimate=pl.CostEstimate(
            flops=2 * slots * edge * edge * classes * share // 4,
            bytes_accessed=2 * slots * edge * edge * share // 4,
            transcendentals=0,
        ),
        name="page_partials",
    )(rows, cols, count, place, tiles, mine, partner)
    return [out[2 * i : 2 * i + 2] for i in range(len(deltas))], out[-1]


def shift(x, axis, by):
    return lax.ppermute(x, axis, [(i, (i + by) % 4) for i in range(4)])


def ring_terms(pieces, axis):
    far_up = shift(pieces[2][0], axis, 1)
    far_down = shift(pieces[2][1], axis, 3)
    near_up = shift(pieces[1][1], axis, 1)
    near_down = shift(pieces[3][0], axis, 3)
    up = shift(add(far_up, pieces[1][0]).astype(BF16), axis, 1)
    down = shift(add(far_down, pieces[3][1]).astype(BF16), axis, 3)
    return (pieces[0][0], near_down, up), (pieces[0][1], near_up, down)


def final_kernel(scale, base, straight, a0, a1, a2, b0, b1, b2, out):
    half = straight.shape[1]
    per = a0.shape[0]

    def put(unit, sums):
        rows = pl.ds(unit * half, half)
        out[rows, :] = (sums * scale[rows, :] + base[rows, :].astype(F32)).astype(BF16)

    put(0, add(*[straight[i] for i in range(4)]))
    for k in range(per):
        put(1 if k == 0 else 2 * k, add(a0[k], a1[k], a2[k]))
        if k:
            put(2 * k + 1, add(b0[k - 1], b1[k - 1], b2[k - 1]))


def local(
    page_scores,
    tile_values,
    tile_row,
    tile_col,
    tile_count,
    page_seed,
    page_label,
    page_degree,
    feature_seed,
    feature_label,
    feature_degree,
):
    tiles = tile_values[0, 0]
    rows, cols = tile_row[0, 0], tile_col[0, 0]
    count = tile_count[0]
    edge = tiles.shape[-1]
    half = edge // 2
    feats, classes = feature_seed.shape[0], page_scores.shape[1]
    page_tiles = page_scores.shape[0] // edge
    per = page_tiles // 16
    place = jnp.stack([lax.axis_index(a) for a in ("x", "zhi", "core")]).astype(jnp.int32)

    def swap(x):
        return lax.ppermute(x, "core", [(0, 1), (1, 0)])

    kept, other = feature_partials(rows, cols, count, place, tiles, page_scores, feats)
    pair = add(kept, swap(other)).astype(BF16)
    parts = lax.all_to_all(pair, CHIPS, 0, 0)
    first = lax.axis_index(ROW) * half

    def own(x):
        return lax.dynamic_slice_in_dim(x, first, half, 0)

    scores = clamp(
        parts.astype(F32).sum(0), own(feature_degree), own(feature_seed), own(feature_label)
    )
    mine = lax.all_to_all(jnp.broadcast_to(scores[None], pair.shape), CHIPS, 0, 0)
    partner = swap(mine)

    known = (page_seed == 1)[:, None]
    hot = page_label[:, None] == lax.broadcasted_iota(jnp.int32, (per * edge, classes), 1)
    base = jnp.where(jnp.logical_and(known, hot), 1.0, 0.0).astype(BF16)
    scale = jnp.where(known, 0.0, lax.rsqrt(page_degree.astype(F32))[:, None])
    scale = jnp.broadcast_to(scale, base.shape)

    def pages(deltas, straight, mine, partner):
        return page_partials(
            deltas, straight, rows, cols, count, place, tiles, mine, partner, page_tiles
        )

    (far,), _ = pages((2,), False, mine, partner)
    (ahead, behind), straight = pages((1, 3), True, mine, partner)
    straight = lax.all_to_all(straight, "zhi", 0, 0)
    far_up = shift(far[0], "x", 1)
    far_down = shift(far[1], "x", 3)
    near_up = shift(ahead[1], "x", 1)
    near_down = shift(behind[0], "x", 3)
    up = add(far_up, ahead[0]).astype(BF16)
    down = add(far_down, behind[1]).astype(BF16)
    up, down, mine, partner = lax.optimization_barrier((up, down, mine, partner))
    up = shift(up, "x", 1)
    down = shift(down, "x", 3)
    (here,), _ = pages((0,), False, mine, partner)
    base, scale, here = lax.optimization_barrier((base, scale, here))
    halves = [
        add(here[0], near_down, up).astype(BF16),
        add(here[1], near_up, down).astype(BF16),
    ]
    straight = lax.all_to_all(straight.astype(F32).sum(0).astype(BF16), "x", 0, 0)
    even, odd = ring_terms([[h[d] for h in halves] for d in range(4)], "zhi")

    return pl.pallas_call(
        final_kernel,
        out_shape=jax.ShapeDtypeStruct(base.shape, BF16),
        in_specs=[VMEM] * 9,
        out_specs=VMEM,
        name="final_sums",
    )(scale, base, straight, *even, *odd)


def solution(mesh):
    parts = Mesh(mesh.devices.reshape(2, 4, 2, 4, 4), ROW + COL)
    in_specs = (
        P(ROW, None),
        P(ROW, COL, None, None, None),
        P(ROW, COL, None),
        P(ROW, COL, None),
        P(ROW, COL),
        P(ROW + COL),
        P(ROW + COL),
        P(ROW + COL),
        P(COL),
        P(COL),
        P(COL),
    )
    return jax.shard_map(
        local, mesh=parts, in_specs=in_specs, out_specs=P(ROW + COL, None), check_vma=False
    )
```

profile of v0, /device:TPU:1, one launch (start us, length us, event | category | flops | bytes accessed | tf_op | source)
XLA Modules:
  0.0 136.8 jit_solution(5796489575183267905)
XLA Ops:
  0.7 0.1 pad_add_fusion.place
  0.7 0.7 copy-done
  1.4 0.7 copy-done.2
  2.0 5.4 %feature_partials.1 = (f32[8,256,128]{2,1,0:T(8,128)S(1)}, f32[8,256,128]{2,1,0:T(8,128)S(1)}) custom-call(s32[22]{0:T(128)S(1)} %bitcast.33, s32[22]{0:T(128)S(1)} %bitcast.37, s32[1]{0:T(128)} %bitcast.29.count_ref, s32[3]{0:T(128)S(1)} %pad_add_fusion.place, bf16[22,512,512]{2,1,0:T(8,128)(2,1)} %bitcast.41, bf16[24576,128]{1,0:T(8,128)(2,1)} %pages.1), custom_call_target="tpu_custom_call" | custom-call | flops 1476395008 | bytes 14417920 | tf_op jit(solution)/shard_map/feature_partials/pallas_call | solution.py:80
  7.5 6.6 %collective-permute-start = (f32[8,256,128]{2,1,0:T(8,128)S(1)}, f32[8,256,128]{2,1,0:T(8,128)S(1)}, u32[]{:S(2)}, u32[]{:S(2)}) collective-permute-start(f32[8,256,128]{2,1,0:T(8,128)S(1)} %get-tuple-element.25), channel_id=1, source_target_pairs={{0,16},{16,0},{1,17},{17,1},{2,18},{18,2},{3,19},{19,3},{4,20},{20... | collective-permute-start | bytes 3145736 | tf_op jit(solution)/shard_map/ppermute | solution.py:295
  14.1 2.3 %collective-permute-done = f32[8,256,128]{2,1,0:T(8,128)S(1)} collective-permute-done((f32[8,256,128]{2,1,0:T(8,128)S(1)}, f32[8,256,128]{2,1,0:T(8,128)S(1)}, u32[]{:S(2)}, u32[]{:S(2)}) %collective-permute-start) | collective-permute-done | bytes 1048608 | tf_op jit(solution)/shard_map/ppermute | solution.py:295
  16.4 0.9 add_convert_fusion.4
  17.3 3.6 %all-to-all-start = ((bf16[8,256,128]{2,1,0:T(8,128)(2,1)}), bf16[8,256,128]{2,1,0:T(8,128)(2,1)S(1)}, u32[]{:S(2)}, u32[]{:S(2)}) async-start(bf16[8,256,128]{2,1,0:T(8,128)(2,1)} %add_convert_fusion.4), calls=%async_computation | async-start | bytes 1048576 | tf_op jit(solution)/shard_map/all_to_all | solution.py:299
  21.0 0.8 dynamic_slice.10
  21.7 0.8 dynamic-slice_compare_fusion
  22.5 0.8 convert_rsqrt_fusion
  23.3 6.1 %all-to-all-done = bf16[8,256,128]{2,1,0:T(8,128)(2,1)S(1)} async-done(((bf16[8,256,128]{2,1,0:T(8,128)(2,1)}), bf16[8,256,128]{2,1,0:T(8,128)(2,1)S(1)}, u32[]{:S(2)}, u32[]{:S(2)}) %all-to-all-start) | async-done | bytes 524320 | tf_op jit(solution)/shard_map/all_to_all | solution.py:299
  29.4 0.1 convert_reduce_fusion
  29.4 0.2 select_convert_fusion.1
  29.7 13.0 %all_to_all.20.mine = bf16[8,256,128]{2,1,0:T(8,128)(2,1)S(1)} all-to-all(bf16[8,256,128]{2,1,0:T(8,128)(2,1)S(1)} %broadcast_in_dim.42), channel_id=1, replica_groups=mesh['zlo'=2,'y'=4,'core'=2,'zhi'=4,'x'=4] {'zlo','y'}, dimensions={0} | all-to-all | bytes 1048576 | tf_op jit(solution)/shard_map/all_to_all | solution.py:308
  42.7 2.3 %collective-permute-start.1 = (bf16[8,256,128]{2,1,0:T(8,128)(2,1)S(1)}, bf16[8,256,128]{2,1,0:T(8,128)(2,1)S(1)}, u32[]{:S(2)}, u32[]{:S(2)}) collective-permute-start(bf16[8,256,128]{2,1,0:T(8,128)(2,1)S(1)} %all_to_all.20.mine), channel_id=1, source_target_pairs={{0,16},{16,0},{1,17},{17,1},{2,18},{18,2},{3,19},{19,3},{4,20},{20... | collective-permute-start | bytes 1572872 | tf_op jit(solution)/shard_map/ppermute | solution.py:295
  45.0 1.5 %collective-permute-done.1.partner = bf16[8,256,128]{2,1,0:T(8,128)(2,1)S(1)} collective-permute-done((bf16[8,256,128]{2,1,0:T(8,128)(2,1)S(1)}, bf16[8,256,128]{2,1,0:T(8,128)(2,1)S(1)}, u32[]{:S(2)}, u32[]{:S(2)}) %collective-permute-start.1) | collective-permute-done | bytes 524320 | tf_op jit(solution)/shard_map/ppermute | solution.py:295
  46.6 3.6 %page_partials.3 = (bf16[4,3,256,128]{3,2,1,0:T(8,128)(2,1)}, bf16[4,2,256,128]{3,2,1,0:T(8,128)(2,1)}) custom-call(s32[22]{0:T(128)S(1)} %bitcast.34, s32[22]{0:T(128)S(1)} %bitcast.38, s32[1]{0:T(128)} %bitcast.30.count_ref, s32[3]{0:T(128)S(1)} %pad_add_fusion.place, bf16[22,512,512]{2,1,0:T(8,128)(2,1)} %bitcast.42, ...), custom_call_target="tpu_custom_call" | custom-call | flops 369098752 | bytes 2883584 | tf_op jit(solution)/shard_map/page_partials/pallas_call | solution.py:217
  50.2 2.2 %collective-permute-start.3 = (bf16[4,2,256,128]{3,2,1,0:T(8,128)(2,1)}, bf16[4,2,256,128]{3,2,1,0:T(8,128)(2,1)}, u32[]{:S(2)}, u32[]{:S(2)}) collective-permute-start(bf16[4,2,256,128]{3,2,1,0:T(8,128)(2,1)} %get-tuple-element.28), channel_id=1, source_target_pairs={{0,3},{1,0},{2,1},{3,2},{4,7},{5,4},{6,5},{7,6},{8,11},{9,8},{10,9... | collective-permute-start | bytes 1572872 | tf_op jit(solution)/shard_map/ppermute | solution.py:243
  52.4 0.6 collective-permute-start.2
  53.0 6.5 %page_partials.4 = (bf16[4,3,256,128]{3,2,1,0:T(8,128)(2,1)S(1)}, bf16[4,2,256,128]{3,2,1,0:T(8,128)(2,1)}, bf16[4,3,256,128]{3,2,1,0:T(8,128)(2,1)S(1)}, bf16[4...) custom-call(s32[22]{0:T(128)S(1)} %bitcast.35, s32[22]{0:T(128)S(1)} %bitcast.39, s32[1]{0:T(128)} %bitcast.31.count_ref, ...), custom_call_target="tpu_custom_call" | custom-call | flops 1107296256 | bytes 8650752 | tf_op jit(solution)/shard_map/page_partials/pallas_call | solution.py:217
  59.5 5.9 %collective-permute-start.9 = (bf16[4,2,256,128]{3,2,1,0:T(8,128)(2,1)}, bf16[4,2,256,128]{3,2,1,0:T(8,128)(2,1)}, u32[]{:S(2)}, u32[]{:S(2)}) collective-permute-start(bf16[4,2,256,128]{3,2,1,0:T(8,128)(2,1)} %get-tuple-element.41), channel_id=1, source_target_pairs={{0,1},{1,2},{2,3},{3,0},{4,5},{5,6},{6,7},{7,4},{8,9},{9,10},{10,1... | collective-permute-start | bytes 1572872 | tf_op jit(solution)/shard_map/ppermute | solution.py:243
  65.5 7.8 %all-to-all-start.2 = ((bf16[4,4,256,128]{3,2,1,0:T(8,128)(2,1)}), bf16[4,4,256,128]{3,2,1,0:T(8,128)(2,1)}, u32[]{:S(2)}, u32[]{:S(2)}) async-start(bf16[4,4,256,128]{3,2,1,0:T(8,128)(2,1)} %get-tuple-element.36), calls=%async_computation.2 | async-start | bytes 2097152 | tf_op jit(solution)/shard_map/all_to_all | solution.py:324
  73.2 1.2 add_convert_fusion.3
  74.5 1.4 add_convert_fusion.1
  75.8 1.5 %collective-permute-start.10 = (bf16[4,2,256,128]{3,2,1,0:T(8,128)(2,1)S(1)}, bf16[4,2,256,128]{3,2,1,0:T(8,128)(2,1)S(1)}, u32[]{:S(2)}, u32[]{:S(2)}) collective-permute-start(bf16[4,2,256,128]{3,2,1,0:T(8,128)(2,1)S(1)} %add_convert_fusion.3), channel_id=1, source_target_pairs={{0,3},{1,0},{2,1},{3,2},{4,7},{5,4},{6,5},{7,6},{8,11},{9,8},{10,9... | collective-permute-start | bytes 1572872 | tf_op jit(solution)/shard_map/ppermute | solution.py:243
  77.3 0.1 collective-permute-start.5
  77.4 1.8 %select_convert_fusion.base = bf16[1536,128]{1,0:T(8,128)(2,1)} fusion(s32[1536]{0:T(1024)S(1)} %copy-done.9, pred[1536]{0:T(1024)(128)(4,1)S(1)} %get-tuple-element.44), kind=kLoop, calls=%fused_computation.6 | loop fusion | flops 786432 | bytes 400896 | tf_op jit(solution)/shard_map/convert_element_type | solution.py:313
  79.1 3.8 %page_partials.5 = (bf16[4,3,256,128]{3,2,1,0:T(8,128)(2,1)S(1)}, bf16[4,2,256,128]{3,2,1,0:T(8,128)(2,1)S(1)}) custom-call(s32[22]{0:T(128)S(1)} %bitcast.36, s32[22]{0:T(128)S(1)} %bitcast.40, s32[1]{0:T(128)} %bitcast.32.count_ref, s32[3]{0:T(128)S(1)} %pad_add_fusion.place, bf16[22,512,512]{2,1,0:T(8,128)(2,1)} %bitcast.44, ...), custom_call_target="tpu_custom_call" | custom-call | flops 369098752 | bytes 2883584 | tf_op jit(solution)/shard_map/page_partials/pallas_call | solution.py:217
  82.9 1.2 broadcast_in_dim.40.scale
  84.1 11.9 %collective-permute-done.10 = bf16[4,2,256,128]{3,2,1,0:T(8,128)(2,1)S(1)} collective-permute-done((bf16[4,2,256,128]{3,2,1,0:T(8,128)(2,1)S(1)}, bf16[4,2,256,128]{3,2,1,0:T(8,128)(2,1)S(1)}, u32[]{:S(2)}, u32[]{:S(2)}) %collective-permute-start.10) | collective-permute-done | bytes 524320 | tf_op jit(solution)/shard_map/ppermute | solution.py:243
  95.9 1.2 add_convert_fusion.2
  97.2 3.2 %collective-permute-done.5 = bf16[4,3,256,128]{3,2,1,0:T(8,128)(2,1)S(1)} collective-permute-done((bf16[4,3,256,128]{3,2,1,0:T(8,128)(2,1)S(1)}, bf16[4,3,256,128]{3,2,1,0:T(8,128)(2,1)S(1)}, u32[]{:S(2)}, u32[]{:S(2)}) %collective-permute-start.5) | collective-permute-done | bytes 786464 | tf_op jit(solution)/shard_map/ppermute | solution.py:243
  100.4 1.4 %add_convert_fusion = bf16[4,3,256,128]{3,2,1,0:T(8,128)(2,1)S(1)} fusion(bf16[4,3,256,128]{3,2,1,0:T(8,128)(2,1)S(1)} %collective-permute-done.5, bf16[4,3,256,128]{3,2,1,0:T(8,128)(2,1)} %collective-permute-done.4, bf16[4,3,256,128]{3,2,1,0:T(8,128)(2,1)S(1)} %get-tuple-element.37), kind=kLoop, calls=%fused_computation | loop fusion | flops 2359296 | bytes 3145728 | tf_op jit(solution)/shard_map/convert_element_type | solution.py:337
  101.8 0.7 slice_bitcast_fusion.1
  102.6 4.4 %collective-permute-start.7 = (bf16[3,256,128]{2,1,0:T(8,128)(2,1)S(1)}, bf16[3,256,128]{2,1,0:T(8,128)(2,1)S(1)}, u32[]{:S(2)}, u32[]{:S(2)}) collective-permute-start(bf16[3,256,128]{2,1,0:T(8,128)(2,1)S(1)} %get-tuple-element.45), channel_id=1, source_target_pairs={{0,4},{4,8},{8,12},{12,0},{1,5},{5,9},{9,13},{13,1},{2,6},{6,10},{... | collective-permute-start | bytes 589832 | tf_op jit(solution)/shard_map/ppermute | solution.py:243
  107.0 0.7 slice_bitcast_fusion.5
  107.7 3.9 %collective-permute-start.12 = (bf16[2,256,128]{2,1,0:T(8,128)(2,1)S(1)}, bf16[2,256,128]{2,1,0:T(8,128)(2,1)S(1)}, u32[]{:S(2)}, u32[]{:S(2)}) collective-permute-start(bf16[2,256,128]{2,1,0:T(8,128)(2,1)S(1)} %get-tuple-element.48), channel_id=1, source_target_pairs={{0,12},{4,0},{8,4},{12,8},{1,13},{5,1},{9,5},{13,9},{2,14},{6,2},{... | collective-permute-start | bytes 393224 | tf_op jit(solution)/shard_map/ppermute | solution.py:243
  111.5 3.6 %collective-permute-start.6 = (bf16[3,256,128]{2,1,0:T(8,128)(2,1)S(1)}, bf16[3,256,128]{2,1,0:T(8,128)(2,1)S(1)}, u32[]{:S(2)}, u32[]{:S(2)}) collective-permute-start(bf16[3,256,128]{2,1,0:T(8,128)(2,1)S(1)} %get-tuple-element.46), channel_id=1, source_target_pairs={{0,12},{4,0},{8,4},{12,8},{1,13},{5,1},{9,5},{13,9},{2,14},{6,2},{... | collective-permute-start | bytes 589832 | tf_op jit(solution)/shard_map/ppermute | solution.py:243
  115.1 2.2 %reduce_sum.22 = bf16[4,256,128]{2,1,0:T(8,128)(2,1)} reduce(bf16[4,4,256,128]{3,2,1,0:T(8,128)(2,1)} %all-to-all-done.2, bf16[]{:T(256)} %constant.39.clone.1), dimensions={0}, to_apply=%region_1.2 | reduce | flops 393216 | bytes 1310722 | tf_op jit(solution)/shard_map/reduce_sum | solution.py:340
  117.3 3.4 %all-to-all-start.3 = ((bf16[4,256,128]{2,1,0:T(8,128)(2,1)}), bf16[4,256,128]{2,1,0:T(8,128)(2,1)S(1)}, u32[]{:S(2)}, u32[]{:S(2)}) async-start(bf16[4,256,128]{2,1,0:T(8,128)(2,1)} %reduce_sum.22), calls=%async_computation.3 | async-start | bytes 524288 | tf_op jit(solution)/shard_map/all_to_all | solution.py:340
  120.7 0.7 collective-permute-done.7
  121.4 0.3 collective-permute-start.8
  121.8 3.4 %collective-permute-start.13 = (bf16[2,256,128]{2,1,0:T(8,128)(2,1)S(1)}, bf16[2,256,128]{2,1,0:T(8,128)(2,1)S(1)}, u32[]{:S(2)}, u32[]{:S(2)}) collective-permute-start(bf16[2,256,128]{2,1,0:T(8,128)(2,1)S(1)} %fusion.2), channel_id=1, source_target_pairs={{0,12},{4,0},{8,4},{12,8},{1,13},{5,1},{9,5},{13,9},{2,14},{6,2},{... | collective-permute-start | bytes 393224 | tf_op jit(solution)/shard_map/ppermute | solution.py:243
  125.2 4.2 %collective-permute-done.13.b2 = bf16[2,256,128]{2,1,0:T(8,128)(2,1)S(1)} collective-permute-done((bf16[2,256,128]{2,1,0:T(8,128)(2,1)S(1)}, bf16[2,256,128]{2,1,0:T(8,128)(2,1)S(1)}, u32[]{:S(2)}, u32[]{:S(2)}) %collective-permute-start.13) | collective-permute-done | bytes 131104 | tf_op jit(solution)/shard_map/ppermute | solution.py:243
  129.4 4.1 %collective-permute-done.8.a2 = bf16[3,256,128]{2,1,0:T(8,128)(2,1)S(1)} collective-permute-done((bf16[3,256,128]{2,1,0:T(8,128)(2,1)S(1)}, bf16[3,256,128]{2,1,0:T(8,128)(2,1)S(1)}, u32[]{:S(2)}, u32[]{:S(2)}) %collective-permute-start.8) | collective-permute-done | bytes 196640 | tf_op jit(solution)/shard_map/ppermute | solution.py:243
  133.5 0.6 copy-done.6
  134.2 2.6 %final_sums.1 = bf16[1536,128]{1,0:T(8,128)(2,1)} custom-call(f32[1536,128]{1,0:T(8,128)} %broadcast_in_dim.40.scale, bf16[1536,128]{1,0:T(8,128)(2,1)} %select_convert_fusion.base, bf16[4,256,128]{2,1,0:T(8,128)(2,1)} %copy-done.4, bf16[3,256,128]{2,1,0:T(8,128)(2,1)} %get-tuple-element.47.a0, bf16[3,256,128]{2,1,0:T(8,128)(2,1)} %copy-done.5, ...), custom_call_target="tpu_custom_call" | custom-call | tf_op jit(solution)/shard_map/final_sums/pallas_call | solution.py:343
  (36 shorter events, 0.2 us)
Async XLA Ops:
  0.7 0.7 copy-start
  1.4 0.7 copy-start.2
  7.5 8.9 %collective-permute-start = (f32[8,256,128]{2,1,0:T(8,128)S(1)}, f32[8,256,128]{2,1,0:T(8,128)S(1)}, u32[]{:S(2)}, u32[]{:S(2)}) collective-permute-start(f32[8,256,128]{2,1,0:T(8,128)S(1)} %get-tuple-element.25), channel_id=1, source_target_pairs={{0,16},{16,0},{1,17},{17,1},{2,18},{18,2},{3,19},{19,3},{4,20},{20... | collective-permute-start | bytes 3145736 | tf_op jit(solution)/shard_map/ppermute | solution.py:295
  17.3 29.2 %copy-start.1 = (s32[1,1,22]{2,1,0:T(1,128)S(1)}, s32[1,1,22]{2,1,0:T(1,128)}, u32[]{:S(2)}) copy-start(s32[1,1,22]{2,1,0:T(1,128)} %param.13) | copy-start | bytes 268
  17.3 29.2 %copy-start.3 = (s32[1,1,22]{2,1,0:T(1,128)S(1)}, s32[1,1,22]{2,1,0:T(1,128)}, u32[]{:S(2)}) copy-start(s32[1,1,22]{2,1,0:T(1,128)} %param.14) | copy-start | bytes 268
  17.3 12.0 %all-to-all-start = ((bf16[8,256,128]{2,1,0:T(8,128)(2,1)}), bf16[8,256,128]{2,1,0:T(8,128)(2,1)S(1)}, u32[]{:S(2)}, u32[]{:S(2)}) async-start(bf16[8,256,128]{2,1,0:T(8,128)(2,1)} %add_convert_fusion.4), calls=%async_computation | async-start | bytes 1048576 | tf_op jit(solution)/shard_map/all_to_all | solution.py:299
  42.7 3.9 %collective-permute-start.1 = (bf16[8,256,128]{2,1,0:T(8,128)(2,1)S(1)}, bf16[8,256,128]{2,1,0:T(8,128)(2,1)S(1)}, u32[]{:S(2)}, u32[]{:S(2)}) collective-permute-start(bf16[8,256,128]{2,1,0:T(8,128)(2,1)S(1)} %all_to_all.20.mine), channel_id=1, source_target_pairs={{0,16},{16,0},{1,17},{17,1},{2,18},{18,2},{3,19},{19,3},{4,20},{20... | collective-permute-start | bytes 1572872 | tf_op jit(solution)/shard_map/ppermute | solution.py:295
  50.2 23.0 %collective-permute-start.3 = (bf16[4,2,256,128]{3,2,1,0:T(8,128)(2,1)}, bf16[4,2,256,128]{3,2,1,0:T(8,128)(2,1)}, u32[]{:S(2)}, u32[]{:S(2)}) collective-permute-start(bf16[4,2,256,128]{3,2,1,0:T(8,128)(2,1)} %get-tuple-element.28), channel_id=1, source_target_pairs={{0,3},{1,0},{2,1},{3,2},{4,7},{5,4},{6,5},{7,6},{8,11},{9,8},{10,9... | collective-permute-start | bytes 1572872 | tf_op jit(solution)/shard_map/ppermute | solution.py:243
  52.4 22.1 %collective-permute-start.2 = (bf16[4,3,256,128]{3,2,1,0:T(8,128)(2,1)}, bf16[4,3,256,128]{3,2,1,0:T(8,128)(2,1)}, u32[]{:S(2)}, u32[]{:S(2)}) collective-permute-start(bf16[4,3,256,128]{3,2,1,0:T(8,128)(2,1)} %get-tuple-element.26), channel_id=1, source_target_pairs={{0,1},{1,2},{2,3},{3,0},{4,5},{5,6},{6,7},{7,4},{8,9},{9,10},{10,1... | collective-permute-start | bytes 2359304 | tf_op jit(solution)/shard_map/ppermute | solution.py:243
  59.5 24.5 %collective-permute-start.9 = (bf16[4,2,256,128]{3,2,1,0:T(8,128)(2,1)}, bf16[4,2,256,128]{3,2,1,0:T(8,128)(2,1)}, u32[]{:S(2)}, u32[]{:S(2)}) collective-permute-start(bf16[4,2,256,128]{3,2,1,0:T(8,128)(2,1)} %get-tuple-element.41), channel_id=1, source_target_pairs={{0,1},{1,2},{2,3},{3,0},{4,5},{5,6},{6,7},{7,4},{8,9},{9,10},{10,1... | collective-permute-start | bytes 1572872 | tf_op jit(solution)/shard_map/ppermute | solution.py:243
  65.5 31.7 %collective-permute-start.4 = (bf16[4,3,256,128]{3,2,1,0:T(8,128)(2,1)S(1)}, bf16[4,3,256,128]{3,2,1,0:T(8,128)(2,1)}, u32[]{:S(2)}, u32[]{:S(2)}) collective-permute-start(bf16[4,3,256,128]{3,2,1,0:T(8,128)(2,1)S(1)} %get-tuple-element.38), channel_id=1, source_target_pairs={{0,3},{1,0},{2,1},{3,2},{4,7},{5,4},{6,5},{7,6},{8,11},{9,8},{10,9... | collective-permute-start | bytes 2359304 | tf_op jit(solution)/shard_map/ppermute | solution.py:243
  65.5 49.6 %all-to-all-start.2 = ((bf16[4,4,256,128]{3,2,1,0:T(8,128)(2,1)}), bf16[4,4,256,128]{3,2,1,0:T(8,128)(2,1)}, u32[]{:S(2)}, u32[]{:S(2)}) async-start(bf16[4,4,256,128]{3,2,1,0:T(8,128)(2,1)} %get-tuple-element.36), calls=%async_computation.2 | async-start | bytes 2097152 | tf_op jit(solution)/shard_map/all_to_all | solution.py:324
  74.4 3.0 %copy-start.10 = (s32[1536]{0:T(1024)S(1)}, s32[1536]{0:T(1024)}, u32[]{:S(2)}) copy-start(s32[1536]{0:T(1024)} %param.18) | copy-start | bytes 18436
  74.4 2.9 %copy-start.11 = (s32[1536]{0:T(1024)S(1)}, s32[1536]{0:T(1024)}, u32[]{:S(2)}) copy-start(s32[1536]{0:T(1024)} %param.16) | copy-start | bytes 18436
  74.4 2.9 %copy-start.9 = (s32[1536]{0:T(1024)S(1)}, s32[1536]{0:T(1024)}, u32[]{:S(2)}) copy-start(s32[1536]{0:T(1024)} %param.17) | copy-start | bytes 18436
  75.8 20.1 %collective-permute-start.10 = (bf16[4,2,256,128]{3,2,1,0:T(8,128)(2,1)S(1)}, bf16[4,2,256,128]{3,2,1,0:T(8,128)(2,1)S(1)}, u32[]{:S(2)}, u32[]{:S(2)}) collective-permute-start(bf16[4,2,256,128]{3,2,1,0:T(8,128)(2,1)S(1)} %add_convert_fusion.3), channel_id=1, source_target_pairs={{0,3},{1,0},{2,1},{3,2},{4,7},{5,4},{6,5},{7,6},{8,11},{9,8},{10,9... | collective-permute-start | bytes 1572872 | tf_op jit(solution)/shard_map/ppermute | solution.py:243
  77.3 23.1 %collective-permute-start.5 = (bf16[4,3,256,128]{3,2,1,0:T(8,128)(2,1)S(1)}, bf16[4,3,256,128]{3,2,1,0:T(8,128)(2,1)S(1)}, u32[]{:S(2)}, u32[]{:S(2)}) collective-permute-start(bf16[4,3,256,128]{3,2,1,0:T(8,128)(2,1)S(1)} %add_convert_fusion.1), channel_id=1, source_target_pairs={{0,1},{1,2},{2,3},{3,0},{4,5},{5,6},{6,7},{7,4},{8,9},{9,10},{10,1... | collective-permute-start | bytes 2359304 | tf_op jit(solution)/shard_map/ppermute | solution.py:243
  102.6 18.8 %collective-permute-start.7 = (bf16[3,256,128]{2,1,0:T(8,128)(2,1)S(1)}, bf16[3,256,128]{2,1,0:T(8,128)(2,1)S(1)}, u32[]{:S(2)}, u32[]{:S(2)}) collective-permute-start(bf16[3,256,128]{2,1,0:T(8,128)(2,1)S(1)} %get-tuple-element.45), channel_id=1, source_target_pairs={{0,4},{4,8},{8,12},{12,0},{1,5},{5,9},{9,13},{13,1},{2,6},{6,10},{... | collective-permute-start | bytes 589832 | tf_op jit(solution)/shard_map/ppermute | solution.py:243
  107.7 14.1 %collective-permute-start.12 = (bf16[2,256,128]{2,1,0:T(8,128)(2,1)S(1)}, bf16[2,256,128]{2,1,0:T(8,128)(2,1)S(1)}, u32[]{:S(2)}, u32[]{:S(2)}) collective-permute-start(bf16[2,256,128]{2,1,0:T(8,128)(2,1)S(1)} %get-tuple-element.48), channel_id=1, source_target_pairs={{0,12},{4,0},{8,4},{12,8},{1,13},{5,1},{9,5},{13,9},{2,14},{6,2},{... | collective-permute-start | bytes 393224 | tf_op jit(solution)/shard_map/ppermute | solution.py:243
  111.5 13.7 %collective-permute-start.11 = (bf16[2,256,128]{2,1,0:T(8,128)(2,1)S(1)}, bf16[2,256,128]{2,1,0:T(8,128)(2,1)S(1)}, u32[]{:S(2)}, u32[]{:S(2)}) collective-permute-start(bf16[2,256,128]{2,1,0:T(8,128)(2,1)S(1)} %get-tuple-element.49), channel_id=1, source_target_pairs={{0,4},{4,8},{8,12},{12,0},{1,5},{5,9},{9,13},{13,1},{2,6},{6,10},{... | collective-permute-start | bytes 393224 | tf_op jit(solution)/shard_map/ppermute | solution.py:243
  111.5 17.9 %collective-permute-start.6 = (bf16[3,256,128]{2,1,0:T(8,128)(2,1)S(1)}, bf16[3,256,128]{2,1,0:T(8,128)(2,1)S(1)}, u32[]{:S(2)}, u32[]{:S(2)}) collective-permute-start(bf16[3,256,128]{2,1,0:T(8,128)(2,1)S(1)} %get-tuple-element.46), channel_id=1, source_target_pairs={{0,12},{4,0},{8,4},{12,8},{1,13},{5,1},{9,5},{13,9},{2,14},{6,2},{... | collective-permute-start | bytes 589832 | tf_op jit(solution)/shard_map/ppermute | solution.py:243
  117.3 12.2 %all-to-all-start.3 = ((bf16[4,256,128]{2,1,0:T(8,128)(2,1)}), bf16[4,256,128]{2,1,0:T(8,128)(2,1)S(1)}, u32[]{:S(2)}, u32[]{:S(2)}) async-start(bf16[4,256,128]{2,1,0:T(8,128)(2,1)} %reduce_sum.22), calls=%async_computation.3 | async-start | bytes 524288 | tf_op jit(solution)/shard_map/all_to_all | solution.py:340
  121.4 12.1 %collective-permute-start.8 = (bf16[3,256,128]{2,1,0:T(8,128)(2,1)S(1)}, bf16[3,256,128]{2,1,0:T(8,128)(2,1)S(1)}, u32[]{:S(2)}, u32[]{:S(2)}) collective-permute-start(bf16[3,256,128]{2,1,0:T(8,128)(2,1)S(1)} %fusion.1), channel_id=1, source_target_pairs={{0,4},{4,8},{8,12},{12,0},{1,5},{5,9},{9,13},{13,1},{2,6},{6,10},{... | collective-permute-start | bytes 589832 | tf_op jit(solution)/shard_map/ppermute | solution.py:243
  121.8 7.6 %collective-permute-start.13 = (bf16[2,256,128]{2,1,0:T(8,128)(2,1)S(1)}, bf16[2,256,128]{2,1,0:T(8,128)(2,1)S(1)}, u32[]{:S(2)}, u32[]{:S(2)}) collective-permute-start(bf16[2,256,128]{2,1,0:T(8,128)(2,1)S(1)} %fusion.2), channel_id=1, source_target_pairs={{0,12},{4,0},{8,4},{12,8},{1,13},{5,1},{9,5},{13,9},{2,14},{6,2},{... | collective-permute-start | bytes 393224 | tf_op jit(solution)/shard_map/ppermute | solution.py:243
  125.2 8.3 %copy-start.7 = (bf16[2,256,128]{2,1,0:T(8,128)(2,1)}, bf16[2,256,128]{2,1,0:T(8,128)(2,1)S(1)}, u32[]{:S(2)}) copy-start(bf16[2,256,128]{2,1,0:T(8,128)(2,1)S(1)} %collective-permute-done.11.b1) | copy-start | bytes 393220
  129.4 4.1 %copy-start.8 = (bf16[2,256,128]{2,1,0:T(8,128)(2,1)}, bf16[2,256,128]{2,1,0:T(8,128)(2,1)S(1)}, u32[]{:S(2)}) copy-start(bf16[2,256,128]{2,1,0:T(8,128)(2,1)S(1)} %collective-permute-done.13.b2) | copy-start | bytes 393220
  129.4 4.1 %copy-start.5 = (bf16[3,256,128]{2,1,0:T(8,128)(2,1)}, bf16[3,256,128]{2,1,0:T(8,128)(2,1)S(1)}, u32[]{:S(2)}) copy-start(bf16[3,256,128]{2,1,0:T(8,128)(2,1)S(1)} %collective-permute-done.6.a1) | copy-start | bytes 589828
  129.4 4.1 %copy-start.4 = (bf16[4,256,128]{2,1,0:T(8,128)(2,1)}, bf16[4,256,128]{2,1,0:T(8,128)(2,1)S(1)}, u32[]{:S(2)}) copy-start(bf16[4,256,128]{2,1,0:T(8,128)(2,1)S(1)} %all-to-all-done.3.straight) | copy-start | bytes 786436
  133.5 0.7 copy-start.6
where the time goes:
time: 139 us; the launch traced here: 137 us
  starting transfers between devices  49.7 us (36%)
  waiting for transfers between devices  34 us (24%)
  Pallas kernels  21.9 us (16%)
  blocking collectives  13 us (9%)
  other arithmetic  12 us (9%)
  local copies, waits for them, and re-layouts  5.36 us (4%)
    ppermute x12, starting transfers between devices, shift(): return lax.ppermute(x, axis, [(i, (i + by) % 4) for i in range(4)])  25.9 us
    ppermute x12, waiting for transfers between devices, shift(): return lax.ppermute(x, axis, [(i, (i + by) % 4) for i in range(4)])  24.1 us
    pallas_call x3, Pallas kernels, page_partials(): pl.pallas_call(functools.partial(page_kernel, deltas, straight, per), out...  13.9 us
    all_to_all x1, blocking collectives, local(): lax.all_to_all(jnp.broadcast_to(scores[None], pair.shape), CHIPS, 0, 0)  13 us
    ppermute x2, starting transfers between devices, swap(): return lax.ppermute(x, 'core', [(0, 1), (1, 0)])  8.97 us
    all_to_all x1, starting transfers between devices, local(): straight = lax.all_to_all(straight, 'zhi', 0, 0)  7.76 us
    all_to_all x1, waiting for transfers between devices, local(): parts = lax.all_to_all(pair, CHIPS, 0, 0)  6.11 us
    pallas_call x1, Pallas kernels, feature_partials(): pl.pallas_call(feature_kernel, out_shape=[halves, halves], in_specs=[SMEM...  5.45 us
  transfers between devices with their start and end apart: 17, of which 8 were waited for; matrix products, arithmetic and copies ran while one was open for 10% of the time, Pallas kernels for 7%

commit v1 on v0

--- a/solution.py
+++ b/solution.py
@@ -34,15 +34,15 @@
 
 
 def feature_kernel(
-    row_ref, col_ref, count_ref, place, tiles, pages, own, other, tile_buf, page_buf, acc, sems
+    table, tiles, pages, own, other, tile_buf, page_buf, acc, sems
 ):
-    edge = tile_buf.shape[1]
+    slots, edge, _ = tile_buf.shape
     half = edge // 2
-    count = count_ref[0]
-    core = place[2]
+    count = table[2 * slots]
+    core = table[2 * slots + 3]
 
     def copies(slot):
-        src = pl.multiple_of(row_ref[slot] * edge, edge)
+        src = pl.multiple_of(table[slot] * edge, edge)
         return (
             pltpu.make_async_copy(tiles.at[slot], tile_buf.at[slot], sems.at[0, slot]),
             pltpu.make_async_copy(pages.at[pl.ds(src, edge)], page_buf.at[slot], sems.at[1, slot]),
@@ -59,7 +59,7 @@
     def _(slot):
         for copy in copies(slot):
             copy.wait()
-        acc[col_ref[slot]] += lax.dot_general(
+        acc[table[slots + slot]] += lax.dot_general(
             page_buf[slot], tile_buf[slot], TILE_T_DOT, preferred_element_type=F32
         )
 
@@ -73,14 +73,14 @@
                 high[tile] = acc[tile, :, half:].T
 
 
-def feature_partials(rows, cols, count, place, tiles, pages, feats):
+def feature_partials(table, tiles, pages, feats):
     slots, edge, _ = tiles.shape
     classes = pages.shape[1]
     halves = jax.ShapeDtypeStruct((feats // edge, edge // 2, classes), F32)
     return pl.pallas_call(
         feature_kernel,
         out_shape=[halves, halves],
-        in_specs=[SMEM] * 4 + [HBM] * 2,
+        in_specs=[SMEM] + [HBM] * 2,
         out_specs=[VMEM] * 2,
         scratch_shapes=[
             pltpu.VMEM((slots, edge, edge), BF16),
@@ -95,21 +95,21 @@
             transcendentals=0,
         ),
         name="feature_partials",
-    )(rows, cols, count, place, tiles, pages)
-
-
-def page_kernel(deltas, straight, per, row_ref, col_ref, count_ref, place, tiles, mine, partner, *rest):
+    )(table, tiles, pages)
+
+
+def page_kernel(deltas, straight, per, table, tiles, mine, partner, *rest):
     n_out = 2 * len(deltas)
     outs, rest = rest[:n_out], rest[n_out:]
     if straight:
         first_out, rest = rest[0], rest[1:]
     tile_buf, feats, acc, head, nxt, sems, feat_sems = rest
-    edge = tile_buf.shape[1]
+    slots, edge, _ = tile_buf.shape
     half = edge // 2
     span = 4 * per
     page_tiles = head.shape[0]
-    count = count_ref[0]
-    core = place[2]
+    count = table[2 * slots]
+    core = table[2 * slots + 3]
 
     def feature_copies():
         for which, source in ((core, mine), (1 - core, partner)):
@@ -128,10 +128,10 @@
 
     @pl.loop(0, count)
     def _(slot):
-        r = row_ref[slot]
+        r = table[slot]
         owner, k = r // per, lax.rem(r, per)
-        ahead = lax.rem(lax.rem(owner, 4) - place[0] + 4, 4)
-        r = ahead * span + lax.rem(owner // 4 - place[1] + 4, 4) * per + k
+        ahead = lax.rem(lax.rem(owner, 4) - table[2 * slots + 1] + 4, 4)
+        r = ahead * span + lax.rem(owner // 4 - table[2 * slots + 2] + 4, 4) * per + k
         wanted = functools.reduce(jnp.logical_or, [ahead == d for d in deltas])
         if straight:
             wanted = jnp.logical_or(wanted, k == 0)
@@ -153,7 +153,7 @@
     def product(slot):
         tile_copy(slot).wait()
         return lax.dot_general(
-            tile_buf[slot], feats[col_ref[slot]], TILE_DOT, preferred_element_type=F32
+            tile_buf[slot], feats[table[slots + slot]], TILE_DOT, preferred_element_type=F32
         )
 
     def visit(delta, index, j):
@@ -173,9 +173,8 @@
 
                 @pl.when(k == 0)
                 def _():
-                    slow = lax.rem(place[1] + second, 4)
-                    fast = lax.rem(place[0] + delta, 4)
-                    first_out[slow, fast] = acc[:half, :].astype(BF16)
+                    slow = lax.rem(table[2 * slots + 2] + second, 4)
+                    first_out[slow, delta] = acc[:half, :].astype(BF16)
 
             for i in range(len(deltas)):
 
@@ -205,7 +204,7 @@
             visit(delta, i * step, j)
 
 
-def page_partials(deltas, straight, rows, cols, count, place, tiles, mine, partner, page_tiles):
+def page_partials(deltas, straight, table, tiles, mine, partner, page_tiles):
     slots, edge, _ = tiles.shape
     classes = mine.shape[-1]
     per = page_tiles // 16
@@ -217,7 +216,7 @@
     out = pl.pallas_call(
         functools.partial(page_kernel, deltas, straight, per),
         out_shape=[jax.ShapeDtypeStruct(s, BF16) for s in shapes],
-        in_specs=[SMEM] * 4 + [HBM] * 3,
+        in_specs=[SMEM] + [HBM] * 3,
         out_specs=[VMEM] * len(shapes),
         scratch_shapes=[
             pltpu.VMEM((slots, edge, edge), BF16),
@@ -235,7 +234,7 @@
             transcendentals=0,
         ),
         name="page_partials",
-    )(rows, cols, count, place, tiles, mine, partner)
+    )(table, tiles, mine, partner)
     return [out[2 * i : 2 * i + 2] for i in range(len(deltas))], out[-1]
 
 
@@ -253,19 +252,39 @@
     return (pieces[0][0], near_down, up), (pieces[0][1], near_up, down)
 
 
-def final_kernel(scale, base, straight, a0, a1, a2, b0, b1, b2, out):
-    half = straight.shape[1]
+def final_kernel(scale, base, s0, s1, s2, s3, a0, a1, a2, b0, b1, b2, out):
+    half = s0.shape[0]
     per = a0.shape[0]
 
     def put(unit, sums):
         rows = pl.ds(unit * half, half)
         out[rows, :] = (sums * scale[rows, :] + base[rows, :].astype(F32)).astype(BF16)
 
-    put(0, add(*[straight[i] for i in range(4)]))
+    put(0, add(s0[...], s1[...], s2[...], s3[...]))
     for k in range(per):
         put(1 if k == 0 else 2 * k, add(a0[k], a1[k], a2[k]))
         if k:
             put(2 * k + 1, add(b0[k - 1], b1[k - 1], b2[k - 1]))
+
+
+def split_kernel(a, b, c, *outs):
+    for d in range(4):
+        outs[d][...] = add(a[d], b[d], c[d]).astype(BF16)
+
+
+def split_sums(*terms):
+    piece = jax.ShapeDtypeStruct(terms[0].shape[1:], BF16)
+    return pl.pallas_call(
+        split_kernel,
+        out_shape=[piece] * 4,
+        in_specs=[VMEM] * 3,
+        out_specs=[VMEM] * 4,
+        compiler_params=pltpu.CompilerParams(vmem_limit_bytes=16 << 20),
+        cost_estimate=pl.CostEstimate(
+            flops=2 * terms[0].size, bytes_accessed=8 * terms[0].size, transcendentals=0
+        ),
+        name="split_sums",
+    )(*terms)
 
 
 def local(
@@ -282,19 +301,18 @@
     feature_degree,
 ):
     tiles = tile_values[0, 0]
-    rows, cols = tile_row[0, 0], tile_col[0, 0]
-    count = tile_count[0]
     edge = tiles.shape[-1]
     half = edge // 2
     feats, classes = feature_seed.shape[0], page_scores.shape[1]
     page_tiles = page_scores.shape[0] // edge
     per = page_tiles // 16
     place = jnp.stack([lax.axis_index(a) for a in ("x", "zhi", "core")]).astype(jnp.int32)
+    table = jnp.concatenate([tile_row[0, 0], tile_col[0, 0], tile_count[0], place])
 
     def swap(x):
         return lax.ppermute(x, "core", [(0, 1), (1, 0)])
 
-    kept, other = feature_partials(rows, cols, count, place, tiles, page_scores, feats)
+    kept, other = feature_partials(table, tiles, page_scores, feats)
     pair = add(kept, swap(other)).astype(BF16)
     parts = lax.all_to_all(pair, CHIPS, 0, 0)
     first = lax.axis_index(ROW) * half
@@ -316,7 +334,7 @@
 
     def pages(deltas, straight, mine, partner):
         return page_partials(
-            deltas, straight, rows, cols, count, place, tiles, mine, partner, page_tiles
+            deltas, straight, table, tiles, mine, partner, page_tiles
         )
 
     (far,), _ = pages((2,), False, mine, partner)
@@ -333,20 +351,19 @@
     down = shift(down, "x", 3)
     (here,), _ = pages((0,), False, mine, partner)
     base, scale, here = lax.optimization_barrier((base, scale, here))
-    halves = [
-        add(here[0], near_down, up).astype(BF16),
-        add(here[1], near_up, down).astype(BF16),
-    ]
-    straight = lax.all_to_all(straight.astype(F32).sum(0).astype(BF16), "x", 0, 0)
+    halves = [split_sums(here[0], near_down, up), split_sums(here[1], near_up, down)]
+    straight = add(*[straight[i] for i in range(4)]).astype(BF16)
+    straight = [straight[0]] + [shift(straight[d], "x", d) for d in (1, 3, 2)]
     even, odd = ring_terms([[h[d] for h in halves] for d in range(4)], "zhi")
 
     return pl.pallas_call(
         final_kernel,
         out_shape=jax.ShapeDtypeStruct(base.shape, BF16),
-        in_specs=[VMEM] * 9,
+        in_specs=[VMEM] * 12,
         out_specs=VMEM,
+        compiler_params=pltpu.CompilerParams(vmem_limit_bytes=16 << 20),
         name="final_sums",
-    )(scale, base, straight, *even, *odd)
+    )(scale, base, *straight, *even, *odd)
 
 
 def solution(mesh):

time: 139 us -> 133 us (0.957)
  the two profiles are of different devices: /device:TPU:1 before, /device:TPU:72 now
where the time goes in v1:
time: 133 us; the launch traced here: 131 us
  waiting for transfers between devices  43.4 us (33%)
  starting transfers between devices  41.5 us (31%)
  Pallas kernels  22.2 us (17%)
  blocking collectives  13 us (10%)
  other arithmetic  7.7 us (6%)
  local copies, waits for them, and re-layouts  2.75 us (2%)
    ppermute x15, waiting for transfers between devices, shift(): return lax.ppermute(x, axis, [(i, (i + by) % 4) for i in range(4)])  32.6 us
    ppermute x15, starting transfers between devices, shift(): return lax.ppermute(x, axis, [(i, (i + by) % 4) for i in range(4)])  26.4 us
    pallas_call x3, Pallas kernels, page_partials(): pl.pallas_call(functools.partial(page_kernel, deltas, straight, per), out...  14.9 us
    all_to_all x1, blocking collectives, local(): lax.all_to_all(jnp.broadcast_to(scores[None], pair.shape), CHIPS, 0, 0)  13 us
    all_to_all x1, starting transfers between devices, local(): parts = lax.all_to_all(pair, CHIPS, 0, 0)  8.59 us
    all_to_all x1, starting transfers between devices, local(): straight = lax.all_to_all(straight, 'zhi', 0, 0)  6.37 us
    all_to_all x1, waiting for transfers between devices, local(): parts = lax.all_to_all(pair, CHIPS, 0, 0)  6.26 us
    pallas_call x1, Pallas kernels, feature_partials(): pl.pallas_call(feature_kernel, out_shape=[halves, halves], in_specs=[SMEM...  5.91 us
  transfers between devices with their start and end apart: 19, of which 11 were waited for; matrix products, arithmetic and copies ran while one was open for 6% of the time, Pallas kernels for 9%

profile of v1, /device:TPU:72, one launch (start us, length us, event | category | flops | bytes accessed | tf_op | source)
XLA Modules:
  0.0 131.5 jit_solution(8615363818820561113)
XLA Ops:
  0.7 0.7 concatenate.3.table
  1.4 5.9 %feature_partials.1 = (f32[8,256,128]{2,1,0:T(8,128)S(1)}, f32[8,256,128]{2,1,0:T(8,128)S(1)}) custom-call(s32[48]{0:T(128)S(1)} %concatenate.3.table, bf16[22,512,512]{2,1,0:T(8,128)(2,1)} %bitcast.16, bf16[24576,128]{1,0:T(8,128)(2,1)} %pages.1), custom_call_target="tpu_custom_call" | custom-call | flops 1476395008 | bytes 14417920 | tf_op jit(solution)/shard_map/feature_partials/pallas_call | solution.py:80
  7.3 0.1 collective-permute-start
  7.4 2.6 %collective-permute-done = f32[8,256,128]{2,1,0:T(8,128)S(1)} collective-permute-done((f32[8,256,128]{2,1,0:T(8,128)S(1)}, f32[8,256,128]{2,1,0:T(8,128)S(1)}, u32[]{:S(2)}, u32[]{:S(2)}) %collective-permute-start) | collective-permute-done | bytes 1048608 | tf_op jit(solution)/shard_map/ppermute | solution.py:313
  10.1 0.9 add_convert_fusion.2
  11.0 8.6 %all-to-all-start = ((bf16[8,256,128]{2,1,0:T(8,128)(2,1)}), bf16[8,256,128]{2,1,0:T(8,128)(2,1)S(1)}, u32[]{:S(2)}, u32[]{:S(2)}) async-start(bf16[8,256,128]{2,1,0:T(8,128)(2,1)} %add_convert_fusion.2), calls=%async_computation | async-start | bytes 1048576 | tf_op jit(solution)/shard_map/all_to_all | solution.py:317
  19.6 0.8 dynamic_slice.10
  20.3 0.8 dynamic-slice_compare_fusion
  21.1 0.8 convert_rsqrt_fusion
  21.9 6.3 %all-to-all-done = bf16[8,256,128]{2,1,0:T(8,128)(2,1)S(1)} async-done(((bf16[8,256,128]{2,1,0:T(8,128)(2,1)}), bf16[8,256,128]{2,1,0:T(8,128)(2,1)S(1)}, u32[]{:S(2)}, u32[]{:S(2)}) %all-to-all-start) | async-done | bytes 524320 | tf_op jit(solution)/shard_map/all_to_all | solution.py:317
  28.1 0.1 convert_reduce_fusion
  28.2 0.2 select_convert_fusion.1
  28.4 0.1 broadcast_in_dim.42
  28.4 13.0 %all_to_all.15.mine = bf16[8,256,128]{2,1,0:T(8,128)(2,1)S(1)} all-to-all(bf16[8,256,128]{2,1,0:T(8,128)(2,1)S(1)} %broadcast_in_dim.42), channel_id=1, replica_groups=mesh['zlo'=2,'y'=4,'core'=2,'zhi'=4,'x'=4] {'zlo','y'}, dimensions={0} | all-to-all | bytes 1048576 | tf_op jit(solution)/shard_map/all_to_all | solution.py:326
  41.4 1.9 %collective-permute-done.1.partner = bf16[8,256,128]{2,1,0:T(8,128)(2,1)S(1)} collective-permute-done((bf16[8,256,128]{2,1,0:T(8,128)(2,1)S(1)}, bf16[8,256,128]{2,1,0:T(8,128)(2,1)S(1)}, u32[]{:S(2)}, u32[]{:S(2)}) %collective-permute-start.1) | collective-permute-done | bytes 524320 | tf_op jit(solution)/shard_map/ppermute | solution.py:313
  43.4 4.1 %page_partials.3 = (bf16[4,3,256,128]{3,2,1,0:T(8,128)(2,1)}, bf16[4,2,256,128]{3,2,1,0:T(8,128)(2,1)}) custom-call(s32[48]{0:T(128)S(1)} %concatenate.3.table, bf16[22,512,512]{2,1,0:T(8,128)(2,1)} %bitcast.17, bf16[8,256,128]{2,1,0:T(8,128)(2,1)S(1)} %all_to_all.15.mine, bf16[8,256,128]{2,1,0:T(8,128)(2,1)S(1)} %collective-permute-done.1.partner), custom_call_target="tpu_custom_call" | custom-call | flops 369098752 | bytes 2883584 | tf_op jit(solution)/shard_map/page_partials/pallas_call | solution.py:216
  47.4 4.3 %collective-permute-start.3 = (bf16[4,2,256,128]{3,2,1,0:T(8,128)(2,1)}, bf16[4,2,256,128]{3,2,1,0:T(8,128)(2,1)}, u32[]{:S(2)}, u32[]{:S(2)}) collective-permute-start(bf16[4,2,256,128]{3,2,1,0:T(8,128)(2,1)} %get-tuple-element.36), channel_id=1, source_target_pairs={{0,3},{1,0},{2,1},{3,2},{4,7},{5,4},{6,5},{7,6},{8,11},{9,8},{10,9... | collective-permute-start | bytes 1572872 | tf_op jit(solution)/shard_map/ppermute | solution.py:242
  51.8 7.3 %page_partials.4 = (bf16[4,3,256,128]{3,2,1,0:T(8,128)(2,1)S(1)}, bf16[4,2,256,128]{3,2,1,0:T(8,128)(2,1)S(1)}, bf16[4,3,256,128]{3,2,1,0:T(8,128)(2,1)S(1)}, bf...) custom-call(s32[48]{0:T(128)S(1)} %concatenate.3.table, bf16[22,512,512]{2,1,0:T(8,128)(2,1)} %bitcast.18, ...), custom_call_target="tpu_custom_call" | custom-call | flops 1107296256 | bytes 8650752 | tf_op jit(solution)/shard_map/page_partials/pallas_call | solution.py:216
  59.1 0.9 copy-done
  60.0 6.4 %all-to-all-start.2 = ((bf16[4,4,256,128]{3,2,1,0:T(8,128)(2,1)}), bf16[4,4,256,128]{3,2,1,0:T(8,128)(2,1)}, u32[]{:S(2)}, u32[]{:S(2)}) async-start(bf16[4,4,256,128]{3,2,1,0:T(8,128)(2,1)} %get-tuple-element.44), calls=%async_computation.2 | async-start | bytes 2097152 | tf_op jit(solution)/shard_map/all_to_all | solution.py:342
  66.3 1.2 add_convert_fusion.1
  67.6 6.2 %collective-permute-done.2 = bf16[4,3,256,128]{3,2,1,0:T(8,128)(2,1)} collective-permute-done((bf16[4,3,256,128]{3,2,1,0:T(8,128)(2,1)}, bf16[4,3,256,128]{3,2,1,0:T(8,128)(2,1)}, u32[]{:S(2)}, u32[]{:S(2)}) %collective-permute-start.2) | collective-permute-done | bytes 786464 | tf_op jit(solution)/shard_map/ppermute | solution.py:242
  73.8 1.3 %add_convert_fusion = bf16[4,3,256,128]{3,2,1,0:T(8,128)(2,1)S(1)} fusion(bf16[4,3,256,128]{3,2,1,0:T(8,128)(2,1)S(1)} %get-tuple-element.35, bf16[4,3,256,128]{3,2,1,0:T(8,128)(2,1)} %collective-permute-done.2), kind=kLoop, calls=%fused_computation | loop fusion | flops 1572864 | bytes 2359296 | tf_op jit(solution)/shard_map/convert_element_type | solution.py:347
  75.1 0.1 collective-permute-start.13
  75.2 1.2 collective-permute-start.7
  76.4 1.0 collective-permute-start.8
  77.4 1.1 select_convert_fusion.base
  78.5 3.5 %page_partials.5 = (bf16[4,3,256,128]{3,2,1,0:T(8,128)(2,1)S(1)}, bf16[4,2,256,128]{3,2,1,0:T(8,128)(2,1)S(1)}) custom-call(s32[48]{0:T(128)S(1)} %concatenate.3.table, bf16[22,512,512]{2,1,0:T(8,128)(2,1)} %bitcast.19, bf16[8,256,128]{2,1,0:T(8,128)(2,1)S(1)} %all_to_all.15.mine, bf16[8,256,128]{2,1,0:T(8,128)(2,1)S(1)} %collective-permute-done.1.partner), custom_call_target="tpu_custom_call" | custom-call | flops 369098752 | bytes 2883584 | tf_op jit(solution)/shard_map/page_partials/pallas_call | solution.py:216
  82.0 0.3 broadcast_in_dim.40.scale
  82.3 2.6 %collective-permute-done.12.b = bf16[4,2,256,128]{3,2,1,0:T(8,128)(2,1)S(1)} collective-permute-done((bf16[4,2,256,128]{3,2,1,0:T(8,128)(2,1)S(1)}, bf16[4,2,256,128]{3,2,1,0:T(8,128)(2,1)S(1)}, u32[]{:S(2)}, u32[]{:S(2)}) %collective-permute-start.12) | collective-permute-done | bytes 524320 | tf_op jit(solution)/shard_map/ppermute | solution.py:242
  84.9 5.2 %collective-permute-done.13.c = bf16[4,2,256,128]{3,2,1,0:T(8,128)(2,1)S(1)} collective-permute-done((bf16[4,2,256,128]{3,2,1,0:T(8,128)(2,1)S(1)}, bf16[4,2,256,128]{3,2,1,0:T(8,128)(2,1)S(1)}, u32[]{:S(2)}, u32[]{:S(2)}) %collective-permute-start.13) | collective-permute-done | bytes 524320 | tf_op jit(solution)/shard_map/ppermute | solution.py:242
  90.0 0.2 split_sums.3
  90.2 0.3 collective-permute-start.15
  90.6 3.9 %collective-permute-start.14 = (bf16[2,256,128]{2,1,0:T(8,128)(2,1)S(1)}, bf16[2,256,128]{2,1,0:T(8,128)(2,1)S(1)}, u32[]{:S(2)}, u32[]{:S(2)}) collective-permute-start(bf16[2,256,128]{2,1,0:T(8,128)(2,1)S(1)} %get-tuple-element.56), channel_id=1, source_target_pairs={{0,4},{4,8},{8,12},{12,0},{1,5},{5,9},{9,13},{13,1},{2,6},{6,10},{... | collective-permute-start | bytes 393224 | tf_op jit(solution)/shard_map/ppermute | solution.py:242
  94.5 4.7 %collective-permute-done.15 = bf16[2,256,128]{2,1,0:T(8,128)(2,1)S(1)} collective-permute-done((bf16[2,256,128]{2,1,0:T(8,128)(2,1)S(1)}, bf16[2,256,128]{2,1,0:T(8,128)(2,1)S(1)}, u32[]{:S(2)}, u32[]{:S(2)}) %collective-permute-start.15) | collective-permute-done | bytes 131104 | tf_op jit(solution)/shard_map/ppermute | solution.py:242
  99.2 2.2 %collective-permute-start.16 = (bf16[2,256,128]{2,1,0:T(8,128)(2,1)S(1)}, bf16[2,256,128]{2,1,0:T(8,128)(2,1)S(1)}, u32[]{:S(2)}, u32[]{:S(2)}) collective-permute-start(bf16[2,256,128]{2,1,0:T(8,128)(2,1)S(1)} %add_convert_fusion.5), channel_id=1, source_target_pairs={{0,12},{4,0},{8,4},{12,8},{1,13},{5,1},{9,5},{13,9},{2,14},{6,2},{... | collective-permute-start | bytes 393224 | tf_op jit(solution)/shard_map/ppermute | solution.py:242
  101.4 0.9 collective-permute-done.7.b
  102.3 0.3 split_sums.2
  102.6 5.4 %collective-permute-start.10 = (bf16[3,256,128]{2,1,0:T(8,128)(2,1)S(1)}, bf16[3,256,128]{2,1,0:T(8,128)(2,1)S(1)}, u32[]{:S(2)}, u32[]{:S(2)}) collective-permute-start(bf16[3,256,128]{2,1,0:T(8,128)(2,1)S(1)} %get-tuple-element.50), channel_id=1, source_target_pairs={{0,4},{4,8},{8,12},{12,0},{1,5},{5,9},{9,13},{13,1},{2,6},{6,10},{... | collective-permute-start | bytes 589832 | tf_op jit(solution)/shard_map/ppermute | solution.py:242
  108.0 1.3 %add_convert_fusion.3 = bf16[1,4,256,128]{3,2,1,0:T(8,128)(2,1)S(1)} fusion(bf16[4,4,256,128]{3,2,1,0:T(8,128)(2,1)} %all-to-all-done.2), kind=kLoop, calls=%fused_computation.7 | loop fusion | flops 1048576 | bytes 1310720 | tf_op jit(solution)/shard_map/convert
  109.4 7.2 %collective-permute-done.10 = bf16[3,256,128]{2,1,0:T(8,128)(2,1)S(1)} collective-permute-done((bf16[3,256,128]{2,1,0:T(8,128)(2,1)S(1)}, bf16[3,256,128]{2,1,0:T(8,128)(2,1)S(1)}, u32[]{:S(2)}, u32[]{:S(2)}) %collective-permute-start.10) | collective-permute-done | bytes 196640 | tf_op jit(solution)/shard_map/ppermute | solution.py:242
  116.6 0.1 add_convert_fusion.4
  116.6 4.7 %collective-permute-start.11 = (bf16[3,256,128]{2,1,0:T(8,128)(2,1)S(1)}, bf16[3,256,128]{2,1,0:T(8,128)(2,1)S(1)}, u32[]{:S(2)}, u32[]{:S(2)}) collective-permute-start(bf16[3,256,128]{2,1,0:T(8,128)(2,1)S(1)} %add_convert_fusion.4), channel_id=1, source_target_pairs={{0,4},{4,8},{8,12},{12,0},{1,5},{5,9},{9,13},{13,1},{2,6},{6,10},{... | collective-permute-start | bytes 589832 | tf_op jit(solution)/shard_map/ppermute | solution.py:242
  121.4 0.1 collective-permute-start.4
  121.5 3.2 %collective-permute-start.5 = (bf16[256,128]{1,0:T(8,128)(2,1)S(1)}, bf16[256,128]{1,0:T(8,128)(2,1)S(1)}, u32[]{:S(2)}, u32[]{:S(2)}) collective-permute-start(bf16[256,128]{1,0:T(8,128)(2,1)S(1)} %get-tuple-element.62), channel_id=1, source_target_pairs={{0,3},{1,0},{2,1},{3,2},{4,7},{5,4},{6,5},{7,6},{8,11},{9,8},{10,9... | collective-permute-start | bytes 196616 | tf_op jit(solution)/shard_map/ppermute | solution.py:242
  124.7 2.2 %collective-permute-done.4.s1 = bf16[256,128]{1,0:T(8,128)(2,1)S(1)} collective-permute-done((bf16[256,128]{1,0:T(8,128)(2,1)S(1)}, bf16[256,128]{1,0:T(8,128)(2,1)S(1)}, u32[]{:S(2)}, u32[]{:S(2)}) %collective-permute-start.4) | collective-permute-done | bytes 65568 | tf_op jit(solution)/shard_map/ppermute | solution.py:242
  126.9 3.5 %collective-permute-done.6.s3 = bf16[256,128]{1,0:T(8,128)(2,1)S(1)} collective-permute-done((bf16[256,128]{1,0:T(8,128)(2,1)S(1)}, bf16[256,128]{1,0:T(8,128)(2,1)S(1)}, u32[]{:S(2)}, u32[]{:S(2)}) %collective-permute-start.6) | collective-permute-done | bytes 65568 | tf_op jit(solution)/shard_map/ppermute | solution.py:242
  130.5 1.0 final_sums.1
  (25 shorter events, 0.1 us)
Async XLA Ops:
  7.3 2.7 %collective-permute-start = (f32[8,256,128]{2,1,0:T(8,128)S(1)}, f32[8,256,128]{2,1,0:T(8,128)S(1)}, u32[]{:S(2)}, u32[]{:S(2)}) collective-permute-start(f32[8,256,128]{2,1,0:T(8,128)S(1)} %get-tuple-element.33), channel_id=1, source_target_pairs={{0,16},{16,0},{1,17},{17,1},{2,18},{18,2},{3,19},{19,3},{4,20},{20... | collective-permute-start | bytes 3145736 | tf_op jit(solution)/shard_map/ppermute | solution.py:313
  11.0 17.1 %all-to-all-start = ((bf16[8,256,128]{2,1,0:T(8,128)(2,1)}), bf16[8,256,128]{2,1,0:T(8,128)(2,1)S(1)}, u32[]{:S(2)}, u32[]{:S(2)}) async-start(bf16[8,256,128]{2,1,0:T(8,128)(2,1)} %add_convert_fusion.2), calls=%async_computation | async-start | bytes 1048576 | tf_op jit(solution)/shard_map/all_to_all | solution.py:317
  41.4 1.9 %collective-permute-start.1 = (bf16[8,256,128]{2,1,0:T(8,128)(2,1)S(1)}, bf16[8,256,128]{2,1,0:T(8,128)(2,1)S(1)}, u32[]{:S(2)}, u32[]{:S(2)}) collective-permute-start(bf16[8,256,128]{2,1,0:T(8,128)(2,1)S(1)} %all_to_all.15.mine), channel_id=1, source_target_pairs={{0,16},{16,0},{1,17},{17,1},{2,18},{18,2},{3,19},{19,3},{4,20},{20... | collective-permute-start | bytes 1572872 | tf_op jit(solution)/shard_map/ppermute | solution.py:313
  47.4 18.9 %collective-permute-start.3 = (bf16[4,2,256,128]{3,2,1,0:T(8,128)(2,1)}, bf16[4,2,256,128]{3,2,1,0:T(8,128)(2,1)}, u32[]{:S(2)}, u32[]{:S(2)}) collective-permute-start(bf16[4,2,256,128]{3,2,1,0:T(8,128)(2,1)} %get-tuple-element.36), channel_id=1, source_target_pairs={{0,3},{1,0},{2,1},{3,2},{4,7},{5,4},{6,5},{7,6},{8,11},{9,8},{10,9... | collective-permute-start | bytes 1572872 | tf_op jit(solution)/shard_map/ppermute | solution.py:242
  51.8 22.0 %collective-permute-start.2 = (bf16[4,3,256,128]{3,2,1,0:T(8,128)(2,1)}, bf16[4,3,256,128]{3,2,1,0:T(8,128)(2,1)}, u32[]{:S(2)}, u32[]{:S(2)}) collective-permute-start(bf16[4,3,256,128]{3,2,1,0:T(8,128)(2,1)} %get-tuple-element.34), channel_id=1, source_target_pairs={{0,1},{1,2},{2,3},{3,0},{4,5},{5,6},{6,7},{7,4},{8,9},{9,10},{10,1... | collective-permute-start | bytes 2359304 | tf_op jit(solution)/shard_map/ppermute | solution.py:242
  59.1 0.9 copy-start
  60.0 24.9 %collective-permute-start.12 = (bf16[4,2,256,128]{3,2,1,0:T(8,128)(2,1)S(1)}, bf16[4,2,256,128]{3,2,1,0:T(8,128)(2,1)S(1)}, u32[]{:S(2)}, u32[]{:S(2)}) collective-permute-start(bf16[4,2,256,128]{3,2,1,0:T(8,128)(2,1)S(1)} %get-tuple-element.53), channel_id=1, source_target_pairs={{0,1},{1,2},{2,3},{3,0},{4,5},{5,6},{6,7},{7,4},{8,9},{9,10},{10,1... | collective-permute-start | bytes 1572872 | tf_op jit(solution)/shard_map/ppermute | solution.py:242
  60.0 48.1 %all-to-all-start.2 = ((bf16[4,4,256,128]{3,2,1,0:T(8,128)(2,1)}), bf16[4,4,256,128]{3,2,1,0:T(8,128)(2,1)}, u32[]{:S(2)}, u32[]{:S(2)}) async-start(bf16[4,4,256,128]{3,2,1,0:T(8,128)(2,1)} %get-tuple-element.44), calls=%async_computation.2 | async-start | bytes 2097152 | tf_op jit(solution)/shard_map/all_to_all | solution.py:342
  67.5 7.7 %copy-start.3 = (s32[1536]{0:T(1024)S(1)}, s32[1536]{0:T(1024)}, u32[]{:S(2)}) copy-start(s32[1536]{0:T(1024)} %param.18) | copy-start | bytes 18436
  67.5 7.7 %copy-start.4 = (s32[1536]{0:T(1024)S(1)}, s32[1536]{0:T(1024)}, u32[]{:S(2)}) copy-start(s32[1536]{0:T(1024)} %param.16) | copy-start | bytes 18436
  67.6 7.7 %copy-start.1 = (bf16[4,3,256,128]{3,2,1,0:T(8,128)(2,1)S(1)}, bf16[4,3,256,128]{3,2,1,0:T(8,128)(2,1)}, u32[]{:S(2)}) copy-start(bf16[4,3,256,128]{3,2,1,0:T(8,128)(2,1)} %copy-done) | copy-start | bytes 2359300
  67.6 9.9 %copy-start.2 = (s32[1536]{0:T(1024)S(1)}, s32[1536]{0:T(1024)}, u32[]{:S(2)}) copy-start(s32[1536]{0:T(1024)} %param.17) | copy-start | bytes 18436
  75.1 14.9 %collective-permute-start.13 = (bf16[4,2,256,128]{3,2,1,0:T(8,128)(2,1)S(1)}, bf16[4,2,256,128]{3,2,1,0:T(8,128)(2,1)S(1)}, u32[]{:S(2)}, u32[]{:S(2)}) collective-permute-start(bf16[4,2,256,128]{3,2,1,0:T(8,128)(2,1)S(1)} %add_convert_fusion.1), channel_id=1, source_target_pairs={{0,3},{1,0},{2,1},{3,2},{4,7},{5,4},{6,5},{7,6},{8,11},{9,8},{10,9... | collective-permute-start | bytes 1572872 | tf_op jit(solution)/shard_map/ppermute | solution.py:242
  75.2 27.1 %collective-permute-start.7 = (bf16[4,3,256,128]{3,2,1,0:T(8,128)(2,1)S(1)}, bf16[4,3,256,128]{3,2,1,0:T(8,128)(2,1)S(1)}, u32[]{:S(2)}, u32[]{:S(2)}) collective-permute-start(bf16[4,3,256,128]{3,2,1,0:T(8,128)(2,1)S(1)} %copy-done.1), channel_id=1, source_target_pairs={{0,3},{1,0},{2,1},{3,2},{4,7},{5,4},{6,5},{7,6},{8,11},{9,8},{10,9... | collective-permute-start | bytes 2359304 | tf_op jit(solution)/shard_map/ppermute | solution.py:242
  76.4 25.9 %collective-permute-start.8 = (bf16[4,3,256,128]{3,2,1,0:T(8,128)(2,1)S(1)}, bf16[4,3,256,128]{3,2,1,0:T(8,128)(2,1)S(1)}, u32[]{:S(2)}, u32[]{:S(2)}) collective-permute-start(bf16[4,3,256,128]{3,2,1,0:T(8,128)(2,1)S(1)} %add_convert_fusion), channel_id=1, source_target_pairs={{0,1},{1,2},{2,3},{3,0},{4,5},{5,6},{6,7},{7,4},{8,9},{9,10},{10,1... | collective-permute-start | bytes 2359304 | tf_op jit(solution)/shard_map/ppermute | solution.py:242
  90.2 8.9 %collective-permute-start.15 = (bf16[2,256,128]{2,1,0:T(8,128)(2,1)S(1)}, bf16[2,256,128]{2,1,0:T(8,128)(2,1)S(1)}, u32[]{:S(2)}, u32[]{:S(2)}) collective-permute-start(bf16[2,256,128]{2,1,0:T(8,128)(2,1)S(1)} %get-tuple-element.57), channel_id=1, source_target_pairs={{0,12},{4,0},{8,4},{12,8},{1,13},{5,1},{9,5},{13,9},{2,14},{6,2},{... | collective-permute-start | bytes 393224 | tf_op jit(solution)/shard_map/ppermute | solution.py:242
  90.6 30.9 %collective-permute-start.14 = (bf16[2,256,128]{2,1,0:T(8,128)(2,1)S(1)}, bf16[2,256,128]{2,1,0:T(8,128)(2,1)S(1)}, u32[]{:S(2)}, u32[]{:S(2)}) collective-permute-start(bf16[2,256,128]{2,1,0:T(8,128)(2,1)S(1)} %get-tuple-element.56), channel_id=1, source_target_pairs={{0,4},{4,8},{8,12},{12,0},{1,5},{5,9},{9,13},{13,1},{2,6},{6,10},{... | collective-permute-start | bytes 393224 | tf_op jit(solution)/shard_map/ppermute | solution.py:242
  99.2 25.5 %collective-permute-start.16 = (bf16[2,256,128]{2,1,0:T(8,128)(2,1)S(1)}, bf16[2,256,128]{2,1,0:T(8,128)(2,1)S(1)}, u32[]{:S(2)}, u32[]{:S(2)}) collective-permute-start(bf16[2,256,128]{2,1,0:T(8,128)(2,1)S(1)} %add_convert_fusion.5), channel_id=1, source_target_pairs={{0,12},{4,0},{8,4},{12,8},{1,13},{5,1},{9,5},{13,9},{2,14},{6,2},{... | collective-permute-start | bytes 393224 | tf_op jit(solution)/shard_map/ppermute | solution.py:242
  102.6 14.0 %collective-permute-start.10 = (bf16[3,256,128]{2,1,0:T(8,128)(2,1)S(1)}, bf16[3,256,128]{2,1,0:T(8,128)(2,1)S(1)}, u32[]{:S(2)}, u32[]{:S(2)}) collective-permute-start(bf16[3,256,128]{2,1,0:T(8,128)(2,1)S(1)} %get-tuple-element.50), channel_id=1, source_target_pairs={{0,4},{4,8},{8,12},{12,0},{1,5},{5,9},{9,13},{13,1},{2,6},{6,10},{... | collective-permute-start | bytes 589832 | tf_op jit(solution)/shard_map/ppermute | solution.py:242
  108.0 22.5 %collective-permute-start.9 = (bf16[3,256,128]{2,1,0:T(8,128)(2,1)S(1)}, bf16[3,256,128]{2,1,0:T(8,128)(2,1)S(1)}, u32[]{:S(2)}, u32[]{:S(2)}) collective-permute-start(bf16[3,256,128]{2,1,0:T(8,128)(2,1)S(1)} %get-tuple-element.49), channel_id=1, source_target_pairs={{0,12},{4,0},{8,4},{12,8},{1,13},{5,1},{9,5},{13,9},{2,14},{6,2},{... | collective-permute-start | bytes 589832 | tf_op jit(solution)/shard_map/ppermute | solution.py:242
  116.6 13.8 %collective-permute-start.11 = (bf16[3,256,128]{2,1,0:T(8,128)(2,1)S(1)}, bf16[3,256,128]{2,1,0:T(8,128)(2,1)S(1)}, u32[]{:S(2)}, u32[]{:S(2)}) collective-permute-start(bf16[3,256,128]{2,1,0:T(8,128)(2,1)S(1)} %add_convert_fusion.4), channel_id=1, source_target_pairs={{0,4},{4,8},{8,12},{12,0},{1,5},{5,9},{9,13},{13,1},{2,6},{6,10},{... | collective-permute-start | bytes 589832 | tf_op jit(solution)/shard_map/ppermute | solution.py:242
  121.4 5.6 %collective-permute-start.4 = (bf16[256,128]{1,0:T(8,128)(2,1)S(1)}, bf16[256,128]{1,0:T(8,128)(2,1)S(1)}, u32[]{:S(2)}, u32[]{:S(2)}) collective-permute-start(bf16[256,128]{1,0:T(8,128)(2,1)S(1)} %get-tuple-element.63), channel_id=1, source_target_pairs={{0,1},{1,2},{2,3},{3,0},{4,5},{5,6},{6,7},{7,4},{8,9},{9,10},{10,1... | collective-permute-start | bytes 196616 | tf_op jit(solution)/shard_map/ppermute | solution.py:242
  121.5 5.5 %collective-permute-start.5 = (bf16[256,128]{1,0:T(8,128)(2,1)S(1)}, bf16[256,128]{1,0:T(8,128)(2,1)S(1)}, u32[]{:S(2)}, u32[]{:S(2)}) collective-permute-start(bf16[256,128]{1,0:T(8,128)(2,1)S(1)} %get-tuple-element.62), channel_id=1, source_target_pairs={{0,3},{1,0},{2,1},{3,2},{4,7},{5,4},{6,5},{7,6},{8,11},{9,8},{10,9... | collective-permute-start | bytes 196616 | tf_op jit(solution)/shard_map/ppermute | solution.py:242
  124.7 5.8 %collective-permute-start.6 = (bf16[256,128]{1,0:T(8,128)(2,1)S(1)}, bf16[256,128]{1,0:T(8,128)(2,1)S(1)}, u32[]{:S(2)}, u32[]{:S(2)}) collective-permute-start(bf16[256,128]{1,0:T(8,128)(2,1)S(1)} %get-tuple-element.61), channel_id=1, source_target_pairs={{0,2},{1,3},{2,0},{3,1},{4,6},{5,7},{6,4},{7,5},{8,10},{9,11},{10,... | collective-permute-start | bytes 196616 | tf_op jit(solution)/shard_map/ppermute | solution.py:242

commit v2 on v1

--- a/solution.py
+++ b/solution.py
@@ -14,6 +14,7 @@
 COL = ("zhi", "x")
 TILE_DOT = (((1,), (0,)), ((), ()))
 TILE_T_DOT = (((0,), (0,)), ((), ()))
+CUT = 256
 SMEM = pl.BlockSpec(memory_space=pltpu.SMEM)
 HBM = pl.BlockSpec(memory_space=pl.ANY)
 VMEM = pl.BlockSpec(memory_space=pltpu.VMEM)
@@ -174,18 +175,24 @@
                 @pl.when(k == 0)
                 def _():
                     slow = lax.rem(table[2 * slots + 2] + second, 4)
-                    first_out[slow, delta] = acc[:half, :].astype(BF16)
-
+                    first_out[slow, delta] = acc[:CUT, :].astype(BF16)
+
+            side = (edge - CUT) // 2
             for i in range(len(deltas)):
+                even, odd = outs[2 * i], outs[2 * i + 1]
 
                 @pl.when(jnp.logical_and(j == i, k == 0))
                 def _():
-                    outs[2 * i][second, 0] = acc[half:, :].astype(BF16)
-
-                @pl.when(jnp.logical_and(j == i, k > 0))
+                    even[second, pl.ds(edge, side)] = acc[CUT : CUT + side, :].astype(BF16)
+                    odd[second, pl.ds(edge, side)] = acc[CUT + side :, :].astype(BF16)
+
+                @pl.when(jnp.logical_and(j == i, k == 1))
                 def _():
-                    outs[2 * i][second, k] = acc[:half, :].astype(BF16)
-                    outs[2 * i + 1][second, k - 1] = acc[half:, :].astype(BF16)
+                    even[second, pl.ds(0, edge)] = acc[...].astype(BF16)
+
+                @pl.when(jnp.logical_and(j == i, k == 2))
+                def _():
+                    odd[second, pl.ds(0, edge)] = acc[...].astype(BF16)
 
     others = [d for d in range(4) if d not in deltas] if straight else []
     walk = [(d, j, 1) for j, d in enumerate(deltas)] + [(d, -1, per) for d in others]
@@ -208,10 +215,9 @@
     slots, edge, _ = tiles.shape
     classes = mine.shape[-1]
     per = page_tiles // 16
-    half = edge // 2
-    shapes = [(4, per, half, classes), (4, per - 1, half, classes)] * len(deltas)
+    shapes = [(4, edge + (edge - CUT) // 2, classes)] * (2 * len(deltas))
     if straight:
-        shapes.append((4, 4, half, classes))
+        shapes.append((4, 4, CUT, classes))
     share = len(deltas) + (1 if straight else 0)
     out = pl.pallas_call(
         functools.partial(page_kernel, deltas, straight, per),
@@ -253,18 +259,17 @@
 
 
 def final_kernel(scale, base, s0, s1, s2, s3, a0, a1, a2, b0, b1, b2, out):
-    half = s0.shape[0]
-    per = a0.shape[0]
-
-    def put(unit, sums):
-        rows = pl.ds(unit * half, half)
+    edge = out.shape[0] // 3
+    side = (edge - CUT) // 2
+
+    def put(start, sums):
+        rows = pl.ds(start, sums.shape[0])
         out[rows, :] = (sums * scale[rows, :] + base[rows, :].astype(F32)).astype(BF16)
 
     put(0, add(s0[...], s1[...], s2[...], s3[...]))
-    for k in range(per):
-        put(1 if k == 0 else 2 * k, add(a0[k], a1[k], a2[k]))
-        if k:
-            put(2 * k + 1, add(b0[k - 1], b1[k - 1], b2[k - 1]))
+    for half, terms in ((0, (a0, a1, a2)), (1, (b0, b1, b2))):
+        put(CUT + half * side, add(*[t[pl.ds(edge, side), :] for t in terms]))
+        put((1 + half) * edge, add(*[t[pl.ds(0, edge), :] for t in terms]))
 
 
 def split_kernel(a, b, c, *outs):

time: 133 us -> 132 us (level)
  the two profiles are of different devices: /device:TPU:72 before, /device:TPU:96 now
where the time goes in v2:
time: 132 us; the launch traced here: 131 us
  starting transfers between devices  45.3 us (34%)
  waiting for transfers between devices  43.8 us (33%)
  Pallas kernels  17.4 us (13%)
  blocking collectives  12.8 us (10%)
  other arithmetic  7.77 us (6%)
  local copies, waits for them, and re-layouts  2.71 us (2%)
    ppermute x15, waiting for transfers between devices, shift(): return lax.ppermute(x, axis, [(i, (i + by) % 4) for i in range(4)])  32.7 us
    ppermute x15, starting transfers between devices, shift(): return lax.ppermute(x, axis, [(i, (i + by) % 4) for i in range(4)])  23.1 us
    all_to_all x1, blocking collectives, local(): lax.all_to_all(jnp.broadcast_to(scores[None], pair.shape), CHIPS, 0, 0)  12.8 us
    all_to_all x1, starting transfers between devices, local(): straight = lax.all_to_all(straight, 'zhi', 0, 0)  11.4 us
    pallas_call x3, Pallas kernels, page_partials(): pl.pallas_call(functools.partial(page_kernel, deltas, straight, per), out...  11.4 us
    all_to_all x1, starting transfers between devices, local(): parts = lax.all_to_all(pair, CHIPS, 0, 0)  10.1 us
    all_to_all x1, waiting for transfers between devices, local(): parts = lax.all_to_all(pair, CHIPS, 0, 0)  6.86 us
    pallas_call x1, Pallas kernels, feature_partials(): pl.pallas_call(feature_kernel, out_shape=[halves, halves], in_specs=[SMEM...  4.62 us
  transfers between devices with their start and end apart: 19, of which 10 were waited for; matrix products, arithmetic and copies ran while one was open for 6% of the time, Pallas kernels for 6%

profile of v2, /device:TPU:96, one launch (start us, length us, event | category | flops | bytes accessed | tf_op | source)
XLA Modules:
  0.0 130.6 jit_solution(11514337576435945377)
XLA Ops:
  0.7 0.7 concatenate.3.table
  1.4 4.6 %feature_partials.1 = (f32[8,256,128]{2,1,0:T(8,128)S(1)}, f32[8,256,128]{2,1,0:T(8,128)S(1)}) custom-call(s32[48]{0:T(128)S(1)} %concatenate.3.table, bf16[22,512,512]{2,1,0:T(8,128)(2,1)} %bitcast.16, bf16[24576,128]{1,0:T(8,128)(2,1)} %pages.1), custom_call_target="tpu_custom_call" | custom-call | flops 1476395008 | bytes 14417920 | tf_op jit(solution)/shard_map/feature_partials/pallas_call | solution.py:81
  6.0 0.7 collective-permute-start
  6.7 2.3 %collective-permute-done = f32[8,256,128]{2,1,0:T(8,128)S(1)} collective-permute-done((f32[8,256,128]{2,1,0:T(8,128)S(1)}, f32[8,256,128]{2,1,0:T(8,128)S(1)}, u32[]{:S(2)}, u32[]{:S(2)}) %collective-permute-start) | collective-permute-done | bytes 1048608 | tf_op jit(solution)/shard_map/ppermute | solution.py:318
  9.0 0.9 add_convert_fusion.2
  9.9 10.1 %all-to-all-start = ((bf16[8,256,128]{2,1,0:T(8,128)(2,1)}), bf16[8,256,128]{2,1,0:T(8,128)(2,1)S(1)}, u32[]{:S(2)}, u32[]{:S(2)}) async-start(bf16[8,256,128]{2,1,0:T(8,128)(2,1)} %add_convert_fusion.2), calls=%async_computation | async-start | bytes 1048576 | tf_op jit(solution)/shard_map/all_to_all | solution.py:322
  20.0 0.8 dynamic_slice.10
  20.8 0.8 dynamic-slice_compare_fusion
  21.6 0.8 convert_rsqrt_fusion
  22.3 6.9 %all-to-all-done = bf16[8,256,128]{2,1,0:T(8,128)(2,1)S(1)} async-done(((bf16[8,256,128]{2,1,0:T(8,128)(2,1)}), bf16[8,256,128]{2,1,0:T(8,128)(2,1)S(1)}, u32[]{:S(2)}, u32[]{:S(2)}) %all-to-all-start) | async-done | bytes 524320 | tf_op jit(solution)/shard_map/all_to_all | solution.py:322
  29.2 0.1 convert_reduce_fusion
  29.3 0.2 select_convert_fusion.1
  29.4 0.1 broadcast_in_dim.42
  29.5 12.8 %all_to_all.15.mine = bf16[8,256,128]{2,1,0:T(8,128)(2,1)S(1)} all-to-all(bf16[8,256,128]{2,1,0:T(8,128)(2,1)S(1)} %broadcast_in_dim.42), channel_id=1, replica_groups=mesh['zlo'=2,'y'=4,'core'=2,'zhi'=4,'x'=4] {'zlo','y'}, dimensions={0} | all-to-all | bytes 1048576 | tf_op jit(solution)/shard_map/all_to_all | solution.py:331
  42.4 1.9 %collective-permute-done.1.partner = bf16[8,256,128]{2,1,0:T(8,128)(2,1)S(1)} collective-permute-done((bf16[8,256,128]{2,1,0:T(8,128)(2,1)S(1)}, bf16[8,256,128]{2,1,0:T(8,128)(2,1)S(1)}, u32[]{:S(2)}, u32[]{:S(2)}) %collective-permute-start.1) | collective-permute-done | bytes 524320 | tf_op jit(solution)/shard_map/ppermute | solution.py:318
  44.3 3.7 %page_partials.3 = (bf16[4,640,128]{2,1,0:T(8,128)(2,1)}, bf16[4,640,128]{2,1,0:T(8,128)(2,1)}) custom-call(s32[48]{0:T(128)S(1)} %concatenate.3.table, bf16[22,512,512]{2,1,0:T(8,128)(2,1)} %bitcast.17, bf16[8,256,128]{2,1,0:T(8,128)(2,1)S(1)} %all_to_all.15.mine, bf16[8,256,128]{2,1,0:T(8,128)(2,1)S(1)} %collective-permute-done.1.partner), custom_call_target="tpu_custom_call" | custom-call | flops 369098752 | bytes 2883584 | tf_op jit(solution)/shard_map/page_partials/pallas_call | solution.py:222
  48.0 0.9 collective-permute-start.3
  48.9 1.2 collective-permute-start.2
  50.1 5.2 %page_partials.4 = (bf16[4,640,128]{2,1,0:T(8,128)(2,1)S(1)}, bf16[4,640,128]{2,1,0:T(8,128)(2,1)}, bf16[4,640,128]{2,1,0:T(8,128)(2,1)S(1)}, bf16[4,640,128]{2,1,0:T(8,128)(2,1)S(1)}, bf16[4,4,256,128]{3,2,1,0:T(8,128)(2,1)}) custom-call(s32[48]{0:T(128)S(1)} %concatenate.3.table, bf16[22,512,512]{2,1,0:T(8,128)(2,1)} %bitcast.18, ...), custom_call_target="tpu_custom_call" | custom-call | flops 1107296256 | bytes 8650752 | tf_op jit(solution)/shard_map/page_partials/pallas_call | solution.py:222
  55.3 0.8 copy-done
  56.1 2.2 %collective-permute-start.12 = (bf16[4,640,128]{2,1,0:T(8,128)(2,1)}, bf16[4,640,128]{2,1,0:T(8,128)(2,1)S(1)}, u32[]{:S(2)}, u32[]{:S(2)}) collective-permute-start(bf16[4,640,128]{2,1,0:T(8,128)(2,1)} %get-tuple-element.53), channel_id=1, source_target_pairs={{0,1},{1,2},{2,3},{3,0},{4,5},{5,6},{6,7},{7,4},{8,9},{9,10},{10,1... | collective-permute-start | bytes 1966088 | tf_op jit(solution)/shard_map/ppermute | solution.py:248
  58.3 11.4 %all-to-all-start.2 = ((bf16[4,4,256,128]{3,2,1,0:T(8,128)(2,1)}), bf16[4,4,256,128]{3,2,1,0:T(8,128)(2,1)}, u32[]{:S(2)}, u32[]{:S(2)}) async-start(bf16[4,4,256,128]{3,2,1,0:T(8,128)(2,1)} %get-tuple-element.44), calls=%async_computation.2 | async-start | bytes 2097152 | tf_op jit(solution)/shard_map/all_to_all | solution.py:347
  69.8 1.3 add_convert_fusion
  71.1 1.3 %add_convert_fusion.1 = bf16[4,640,128]{2,1,0:T(8,128)(2,1)S(1)} fusion(bf16[4,640,128]{2,1,0:T(8,128)(2,1)S(1)} %get-tuple-element.35, bf16[4,640,128]{2,1,0:T(8,128)(2,1)} %collective-permute-done.2), kind=kLoop, calls=%fused_computation.1 | loop fusion | flops 1310720 | bytes 1966080 | tf_op jit(solution)/shard_map/convert_element_type | solution.py:352
  72.4 0.1 collective-permute-start.13
  72.5 0.9 collective-permute-start.7
  73.5 1.3 collective-permute-start.8
  74.7 1.1 select_convert_fusion.base
  75.8 2.5 %page_partials.5 = (bf16[4,640,128]{2,1,0:T(8,128)(2,1)S(1)}, bf16[4,640,128]{2,1,0:T(8,128)(2,1)S(1)}) custom-call(s32[48]{0:T(128)S(1)} %concatenate.3.table, bf16[22,512,512]{2,1,0:T(8,128)(2,1)} %bitcast.19, bf16[8,256,128]{2,1,0:T(8,128)(2,1)S(1)} %all_to_all.15.mine, bf16[8,256,128]{2,1,0:T(8,128)(2,1)S(1)} %collective-permute-done.1.partner), custom_call_target="tpu_custom_call" | custom-call | flops 369098752 | bytes 2883584 | tf_op jit(solution)/shard_map/page_partials/pallas_call | solution.py:222
  78.2 0.3 broadcast_in_dim.40.scale
  78.5 1.3 collective-permute-done.12.b
  79.8 10.1 %collective-permute-done.13.c = bf16[4,640,128]{2,1,0:T(8,128)(2,1)S(1)} collective-permute-done((bf16[4,640,128]{2,1,0:T(8,128)(2,1)S(1)}, bf16[4,640,128]{2,1,0:T(8,128)(2,1)S(1)}, u32[]{:S(2)}, u32[]{:S(2)}) %collective-permute-start.13) | collective-permute-done | bytes 655392 | tf_op jit(solution)/shard_map/ppermute | solution.py:248
  89.9 0.2 split_sums.3
  90.1 0.3 collective-permute-start.15
  90.4 3.9 %collective-permute-start.14 = (bf16[640,128]{1,0:T(8,128)(2,1)S(1)}, bf16[640,128]{1,0:T(8,128)(2,1)S(1)}, u32[]{:S(2)}, u32[]{:S(2)}) collective-permute-start(bf16[640,128]{1,0:T(8,128)(2,1)S(1)} %get-tuple-element.56), channel_id=1, source_target_pairs={{0,4},{4,8},{8,12},{12,0},{1,5},{5,9},{9,13},{13,1},{2,6},{6,10},{... | collective-permute-start | bytes 491528 | tf_op jit(solution)/shard_map/ppermute | solution.py:248
  94.3 9.6 %collective-permute-done.7.b = bf16[4,640,128]{2,1,0:T(8,128)(2,1)S(1)} collective-permute-done((bf16[4,640,128]{2,1,0:T(8,128)(2,1)S(1)}, bf16[4,640,128]{2,1,0:T(8,128)(2,1)S(1)}, u32[]{:S(2)}, u32[]{:S(2)}) %collective-permute-start.7) | collective-permute-done | bytes 655392 | tf_op jit(solution)/shard_map/ppermute | solution.py:248
  103.9 0.2 split_sums.2
  104.2 3.4 %collective-permute-start.10 = (bf16[640,128]{1,0:T(8,128)(2,1)S(1)}, bf16[640,128]{1,0:T(8,128)(2,1)S(1)}, u32[]{:S(2)}, u32[]{:S(2)}) collective-permute-start(bf16[640,128]{1,0:T(8,128)(2,1)S(1)} %get-tuple-element.50), channel_id=1, source_target_pairs={{0,4},{4,8},{8,12},{12,0},{1,5},{5,9},{9,13},{13,1},{2,6},{6,10},{... | collective-permute-start | bytes 491528 | tf_op jit(solution)/shard_map/ppermute | solution.py:248
  107.7 0.9 collective-permute-start.16
  108.6 6.0 %collective-permute-done.10 = bf16[640,128]{1,0:T(8,128)(2,1)S(1)} collective-permute-done((bf16[640,128]{1,0:T(8,128)(2,1)S(1)}, bf16[640,128]{1,0:T(8,128)(2,1)S(1)}, u32[]{:S(2)}, u32[]{:S(2)}) %collective-permute-start.10) | collective-permute-done | bytes 163872 | tf_op jit(solution)/shard_map/ppermute | solution.py:248
  114.6 4.6 %collective-permute-start.11 = (bf16[640,128]{1,0:T(8,128)(2,1)S(1)}, bf16[640,128]{1,0:T(8,128)(2,1)S(1)}, u32[]{:S(2)}, u32[]{:S(2)}) collective-permute-start(bf16[640,128]{1,0:T(8,128)(2,1)S(1)} %add_convert_fusion.5), channel_id=1, source_target_pairs={{0,4},{4,8},{8,12},{12,0},{1,5},{5,9},{9,13},{13,1},{2,6},{6,10},{... | collective-permute-start | bytes 491528 | tf_op jit(solution)/shard_map/ppermute | solution.py:248
  119.2 1.3 %add_convert_fusion.3 = bf16[1,4,256,128]{3,2,1,0:T(8,128)(2,1)S(1)} fusion(bf16[4,4,256,128]{3,2,1,0:T(8,128)(2,1)} %all-to-all-done.2), kind=kLoop, calls=%fused_computation.7 | loop fusion | flops 1048576 | bytes 1310720 | tf_op jit(solution)/shard_map/convert
  120.6 0.9 collective-permute-start.4
  121.5 2.4 %collective-permute-start.5 = (bf16[256,128]{1,0:T(8,128)(2,1)S(1)}, bf16[256,128]{1,0:T(8,128)(2,1)S(1)}, u32[]{:S(2)}, u32[]{:S(2)}) collective-permute-start(bf16[256,128]{1,0:T(8,128)(2,1)S(1)} %get-tuple-element.62), channel_id=1, source_target_pairs={{0,3},{1,0},{2,1},{3,2},{4,7},{5,4},{6,5},{7,6},{8,11},{9,8},{10,9... | collective-permute-start | bytes 196616 | tf_op jit(solution)/shard_map/ppermute | solution.py:248
  123.9 2.0 %collective-permute-done.16.b2 = bf16[640,128]{1,0:T(8,128)(2,1)S(1)} collective-permute-done((bf16[640,128]{1,0:T(8,128)(2,1)S(1)}, bf16[640,128]{1,0:T(8,128)(2,1)S(1)}, u32[]{:S(2)}, u32[]{:S(2)}) %collective-permute-start.16) | collective-permute-done | bytes 163872 | tf_op jit(solution)/shard_map/ppermute | solution.py:248
  125.9 0.9 collective-permute-done.4.s1
  126.8 2.8 %collective-permute-done.6.s3 = bf16[256,128]{1,0:T(8,128)(2,1)S(1)} collective-permute-done((bf16[256,128]{1,0:T(8,128)(2,1)S(1)}, bf16[256,128]{1,0:T(8,128)(2,1)S(1)}, u32[]{:S(2)}, u32[]{:S(2)}) %collective-permute-start.6) | collective-permute-done | bytes 65568 | tf_op jit(solution)/shard_map/ppermute | solution.py:248
  129.7 1.0 final_sums.1
  (25 shorter events, 0.2 us)
Async XLA Ops:
  6.0 3.0 %collective-permute-start = (f32[8,256,128]{2,1,0:T(8,128)S(1)}, f32[8,256,128]{2,1,0:T(8,128)S(1)}, u32[]{:S(2)}, u32[]{:S(2)}) collective-permute-start(f32[8,256,128]{2,1,0:T(8,128)S(1)} %get-tuple-element.33), channel_id=1, source_target_pairs={{0,16},{16,0},{1,17},{17,1},{2,18},{18,2},{3,19},{19,3},{4,20},{20... | collective-permute-start | bytes 3145736 | tf_op jit(solution)/shard_map/ppermute | solution.py:318
  9.9 19.3 %all-to-all-start = ((bf16[8,256,128]{2,1,0:T(8,128)(2,1)}), bf16[8,256,128]{2,1,0:T(8,128)(2,1)S(1)}, u32[]{:S(2)}, u32[]{:S(2)}) async-start(bf16[8,256,128]{2,1,0:T(8,128)(2,1)} %add_convert_fusion.2), calls=%async_computation | async-start | bytes 1048576 | tf_op jit(solution)/shard_map/all_to_all | solution.py:322
  42.4 1.9 %collective-permute-start.1 = (bf16[8,256,128]{2,1,0:T(8,128)(2,1)S(1)}, bf16[8,256,128]{2,1,0:T(8,128)(2,1)S(1)}, u32[]{:S(2)}, u32[]{:S(2)}) collective-permute-start(bf16[8,256,128]{2,1,0:T(8,128)(2,1)S(1)} %all_to_all.15.mine), channel_id=1, source_target_pairs={{0,16},{16,0},{1,17},{17,1},{2,18},{18,2},{3,19},{19,3},{4,20},{20... | collective-permute-start | bytes 1572872 | tf_op jit(solution)/shard_map/ppermute | solution.py:318
  48.0 21.8 %collective-permute-start.3 = (bf16[4,640,128]{2,1,0:T(8,128)(2,1)}, bf16[4,640,128]{2,1,0:T(8,128)(2,1)}, u32[]{:S(2)}, u32[]{:S(2)}) collective-permute-start(bf16[4,640,128]{2,1,0:T(8,128)(2,1)} %get-tuple-element.36), channel_id=1, source_target_pairs={{0,3},{1,0},{2,1},{3,2},{4,7},{5,4},{6,5},{7,6},{8,11},{9,8},{10,9... | collective-permute-start | bytes 1966088 | tf_op jit(solution)/shard_map/ppermute | solution.py:248
  48.9 22.2 %collective-permute-start.2 = (bf16[4,640,128]{2,1,0:T(8,128)(2,1)}, bf16[4,640,128]{2,1,0:T(8,128)(2,1)}, u32[]{:S(2)}, u32[]{:S(2)}) collective-permute-start(bf16[4,640,128]{2,1,0:T(8,128)(2,1)} %get-tuple-element.34), channel_id=1, source_target_pairs={{0,1},{1,2},{2,3},{3,0},{4,5},{5,6},{6,7},{7,4},{8,9},{9,10},{10,1... | collective-permute-start | bytes 1966088 | tf_op jit(solution)/shard_map/ppermute | solution.py:248
  55.3 0.8 copy-start
  56.1 23.6 %collective-permute-start.12 = (bf16[4,640,128]{2,1,0:T(8,128)(2,1)}, bf16[4,640,128]{2,1,0:T(8,128)(2,1)S(1)}, u32[]{:S(2)}, u32[]{:S(2)}) collective-permute-start(bf16[4,640,128]{2,1,0:T(8,128)(2,1)} %get-tuple-element.53), channel_id=1, source_target_pairs={{0,1},{1,2},{2,3},{3,0},{4,5},{5,6},{6,7},{7,4},{8,9},{9,10},{10,1... | collective-permute-start | bytes 1966088 | tf_op jit(solution)/shard_map/ppermute | solution.py:248
  58.3 60.9 %all-to-all-start.2 = ((bf16[4,4,256,128]{3,2,1,0:T(8,128)(2,1)}), bf16[4,4,256,128]{3,2,1,0:T(8,128)(2,1)}, u32[]{:S(2)}, u32[]{:S(2)}) async-start(bf16[4,4,256,128]{3,2,1,0:T(8,128)(2,1)} %get-tuple-element.44), calls=%async_computation.2 | async-start | bytes 2097152 | tf_op jit(solution)/shard_map/all_to_all | solution.py:347
  71.0 1.5 %copy-start.3 = (s32[1536]{0:T(1024)S(1)}, s32[1536]{0:T(1024)}, u32[]{:S(2)}) copy-start(s32[1536]{0:T(1024)} %param.18) | copy-start | bytes 18436
  71.0 1.5 %copy-start.4 = (s32[1536]{0:T(1024)S(1)}, s32[1536]{0:T(1024)}, u32[]{:S(2)}) copy-start(s32[1536]{0:T(1024)} %param.16) | copy-start | bytes 18436
  71.0 1.5 %copy-start.1 = (bf16[4,640,128]{2,1,0:T(8,128)(2,1)S(1)}, bf16[4,640,128]{2,1,0:T(8,128)(2,1)}, u32[]{:S(2)}) copy-start(bf16[4,640,128]{2,1,0:T(8,128)(2,1)} %copy-done) | copy-start | bytes 1966084
  71.1 3.7 %copy-start.2 = (s32[1536]{0:T(1024)S(1)}, s32[1536]{0:T(1024)}, u32[]{:S(2)}) copy-start(s32[1536]{0:T(1024)} %param.17) | copy-start | bytes 18436
  72.4 17.5 %collective-permute-start.13 = (bf16[4,640,128]{2,1,0:T(8,128)(2,1)S(1)}, bf16[4,640,128]{2,1,0:T(8,128)(2,1)S(1)}, u32[]{:S(2)}, u32[]{:S(2)}) collective-permute-start(bf16[4,640,128]{2,1,0:T(8,128)(2,1)S(1)} %add_convert_fusion), channel_id=1, source_target_pairs={{0,3},{1,0},{2,1},{3,2},{4,7},{5,4},{6,5},{7,6},{8,11},{9,8},{10,9... | collective-permute-start | bytes 1966088 | tf_op jit(solution)/shard_map/ppermute | solution.py:248
  72.5 31.4 %collective-permute-start.7 = (bf16[4,640,128]{2,1,0:T(8,128)(2,1)S(1)}, bf16[4,640,128]{2,1,0:T(8,128)(2,1)S(1)}, u32[]{:S(2)}, u32[]{:S(2)}) collective-permute-start(bf16[4,640,128]{2,1,0:T(8,128)(2,1)S(1)} %copy-done.1), channel_id=1, source_target_pairs={{0,3},{1,0},{2,1},{3,2},{4,7},{5,4},{6,5},{7,6},{8,11},{9,8},{10,9... | collective-permute-start | bytes 1966088 | tf_op jit(solution)/shard_map/ppermute | solution.py:248
  73.5 30.5 %collective-permute-start.8 = (bf16[4,640,128]{2,1,0:T(8,128)(2,1)S(1)}, bf16[4,640,128]{2,1,0:T(8,128)(2,1)S(1)}, u32[]{:S(2)}, u32[]{:S(2)}) collective-permute-start(bf16[4,640,128]{2,1,0:T(8,128)(2,1)S(1)} %add_convert_fusion.1), channel_id=1, source_target_pairs={{0,1},{1,2},{2,3},{3,0},{4,5},{5,6},{6,7},{7,4},{8,9},{9,10},{10,1... | collective-permute-start | bytes 1966088 | tf_op jit(solution)/shard_map/ppermute | solution.py:248
  90.1 17.5 %collective-permute-start.15 = (bf16[640,128]{1,0:T(8,128)(2,1)S(1)}, bf16[640,128]{1,0:T(8,128)(2,1)S(1)}, u32[]{:S(2)}, u32[]{:S(2)}) collective-permute-start(bf16[640,128]{1,0:T(8,128)(2,1)S(1)} %get-tuple-element.57), channel_id=1, source_target_pairs={{0,12},{4,0},{8,4},{12,8},{1,13},{5,1},{9,5},{13,9},{2,14},{6,2},{... | collective-permute-start | bytes 491528 | tf_op jit(solution)/shard_map/ppermute | solution.py:248
  90.4 31.1 %collective-permute-start.14 = (bf16[640,128]{1,0:T(8,128)(2,1)S(1)}, bf16[640,128]{1,0:T(8,128)(2,1)S(1)}, u32[]{:S(2)}, u32[]{:S(2)}) collective-permute-start(bf16[640,128]{1,0:T(8,128)(2,1)S(1)} %get-tuple-element.56), channel_id=1, source_target_pairs={{0,4},{4,8},{8,12},{12,0},{1,5},{5,9},{9,13},{13,1},{2,6},{6,10},{... | collective-permute-start | bytes 491528 | tf_op jit(solution)/shard_map/ppermute | solution.py:248
  104.2 10.3 %collective-permute-start.10 = (bf16[640,128]{1,0:T(8,128)(2,1)S(1)}, bf16[640,128]{1,0:T(8,128)(2,1)S(1)}, u32[]{:S(2)}, u32[]{:S(2)}) collective-permute-start(bf16[640,128]{1,0:T(8,128)(2,1)S(1)} %get-tuple-element.50), channel_id=1, source_target_pairs={{0,4},{4,8},{8,12},{12,0},{1,5},{5,9},{9,13},{13,1},{2,6},{6,10},{... | collective-permute-start | bytes 491528 | tf_op jit(solution)/shard_map/ppermute | solution.py:248
  107.6 16.3 %collective-permute-start.9 = (bf16[640,128]{1,0:T(8,128)(2,1)S(1)}, bf16[640,128]{1,0:T(8,128)(2,1)S(1)}, u32[]{:S(2)}, u32[]{:S(2)}) collective-permute-start(bf16[640,128]{1,0:T(8,128)(2,1)S(1)} %get-tuple-element.49), channel_id=1, source_target_pairs={{0,12},{4,0},{8,4},{12,8},{1,13},{5,1},{9,5},{13,9},{2,14},{6,2},{... | collective-permute-start | bytes 491528 | tf_op jit(solution)/shard_map/ppermute | solution.py:248
  107.7 18.2 %collective-permute-start.16 = (bf16[640,128]{1,0:T(8,128)(2,1)S(1)}, bf16[640,128]{1,0:T(8,128)(2,1)S(1)}, u32[]{:S(2)}, u32[]{:S(2)}) collective-permute-start(bf16[640,128]{1,0:T(8,128)(2,1)S(1)} %add_convert_fusion.4), channel_id=1, source_target_pairs={{0,12},{4,0},{8,4},{12,8},{1,13},{5,1},{9,5},{13,9},{2,14},{6,2},{... | collective-permute-start | bytes 491528 | tf_op jit(solution)/shard_map/ppermute | solution.py:248
  114.6 11.3 %collective-permute-start.11 = (bf16[640,128]{1,0:T(8,128)(2,1)S(1)}, bf16[640,128]{1,0:T(8,128)(2,1)S(1)}, u32[]{:S(2)}, u32[]{:S(2)}) collective-permute-start(bf16[640,128]{1,0:T(8,128)(2,1)S(1)} %add_convert_fusion.5), channel_id=1, source_target_pairs={{0,4},{4,8},{8,12},{12,0},{1,5},{5,9},{9,13},{13,1},{2,6},{6,10},{... | collective-permute-start | bytes 491528 | tf_op jit(solution)/shard_map/ppermute | solution.py:248
  120.6 6.3 %collective-permute-start.4 = (bf16[256,128]{1,0:T(8,128)(2,1)S(1)}, bf16[256,128]{1,0:T(8,128)(2,1)S(1)}, u32[]{:S(2)}, u32[]{:S(2)}) collective-permute-start(bf16[256,128]{1,0:T(8,128)(2,1)S(1)} %get-tuple-element.63), channel_id=1, source_target_pairs={{0,1},{1,2},{2,3},{3,0},{4,5},{5,6},{6,7},{7,4},{8,9},{9,10},{10,1... | collective-permute-start | bytes 196616 | tf_op jit(solution)/shard_map/ppermute | solution.py:248
  121.5 5.3 %collective-permute-start.5 = (bf16[256,128]{1,0:T(8,128)(2,1)S(1)}, bf16[256,128]{1,0:T(8,128)(2,1)S(1)}, u32[]{:S(2)}, u32[]{:S(2)}) collective-permute-start(bf16[256,128]{1,0:T(8,128)(2,1)S(1)} %get-tuple-element.62), channel_id=1, source_target_pairs={{0,3},{1,0},{2,1},{3,2},{4,7},{5,4},{6,5},{7,6},{8,11},{9,8},{10,9... | collective-permute-start | bytes 196616 | tf_op jit(solution)/shard_map/ppermute | solution.py:248
  123.9 5.8 %collective-permute-start.6 = (bf16[256,128]{1,0:T(8,128)(2,1)S(1)}, bf16[256,128]{1,0:T(8,128)(2,1)S(1)}, u32[]{:S(2)}, u32[]{:S(2)}) collective-permute-start(bf16[256,128]{1,0:T(8,128)(2,1)S(1)} %get-tuple-element.61), channel_id=1, source_target_pairs={{0,2},{1,3},{2,0},{3,1},{4,6},{5,7},{6,4},{7,5},{8,10},{9,11},{10,... | collective-permute-start | bytes 196616 | tf_op jit(solution)/shard_map/ppermute | solution.py:248

commit v3 on v2

--- a/solution.py
+++ b/solution.py
@@ -14,7 +14,7 @@
 COL = ("zhi", "x")
 TILE_DOT = (((1,), (0,)), ((), ()))
 TILE_T_DOT = (((0,), (0,)), ((), ()))
-CUT = 256
+CUT = 224
 SMEM = pl.BlockSpec(memory_space=pltpu.SMEM)
 HBM = pl.BlockSpec(memory_space=pl.ANY)
 VMEM = pl.BlockSpec(memory_space=pltpu.VMEM)

time: 132 us -> 137 us (1.038)
  the two profiles are of different devices: /device:TPU:96 before, /device:TPU:70 now
where the time goes in v3:
time: 137 us
  waiting for transfers between devices  52 us (38%)
  Pallas kernels  30.4 us (22%)
  starting transfers between devices  29.7 us (22%)
  blocking collectives  13.4 us (10%)
  other arithmetic  7.84 us (6%)
  local copies, waits for them, and re-layouts  2.71 us (2%)
    ppermute x15, waiting for transfers between devices, shift(): return lax.ppermute(x, axis, [(i, (i + by) % 4) for i in range(4)])  40 us
    ppermute x15, starting transfers between devices, shift(): return lax.ppermute(x, axis, [(i, (i + by) % 4) for i in range(4)])  21.2 us
    pallas_call x3, Pallas kernels, page_partials(): pl.pallas_call(functools.partial(page_kernel, deltas, straight, per), out...  19.1 us
    all_to_all x1, blocking collectives, local(): lax.all_to_all(jnp.broadcast_to(scores[None], pair.shape), CHIPS, 0, 0)  13.4 us
    pallas_call x1, Pallas kernels, feature_partials(): pl.pallas_call(feature_kernel, out_shape=[halves, halves], in_specs=[SMEM...  9.86 us
    all_to_all x1, waiting for transfers between devices, local(): parts = lax.all_to_all(pair, CHIPS, 0, 0)  7.44 us
    ppermute x2, waiting for transfers between devices, swap(): return lax.ppermute(x, 'core', [(0, 1), (1, 0)])  4.55 us
    all_to_all x1, starting transfers between devices, local(): straight = lax.all_to_all(straight, 'zhi', 0, 0)  4.21 us
  transfers between devices with their start and end apart: 19, of which 9 were waited for; matrix products, arithmetic and copies ran while one was open for 6% of the time, Pallas kernels for 10%

profile of v3, /device:TPU:70, one launch (start us, length us, event | category | flops | bytes accessed | tf_op | source)
XLA Modules:
  0.0 137.0 jit_solution(3161637121525501728)
XLA Ops:
  0.7 0.7 concatenate.3.table
  1.4 9.9 %feature_partials.1 = (f32[8,256,128]{2,1,0:T(8,128)S(1)}, f32[8,256,128]{2,1,0:T(8,128)S(1)}) custom-call(s32[48]{0:T(128)S(1)} %concatenate.3.table, bf16[22,512,512]{2,1,0:T(8,128)(2,1)} %bitcast.16, bf16[24576,128]{1,0:T(8,128)(2,1)} %pages.1), custom_call_target="tpu_custom_call" | custom-call | flops 1476395008 | bytes 14417920 | tf_op jit(solution)/shard_map/feature_partials/pallas_call | solution.py:81
  11.3 0.1 collective-permute-start
  11.4 2.6 %collective-permute-done = f32[8,256,128]{2,1,0:T(8,128)S(1)} collective-permute-done((f32[8,256,128]{2,1,0:T(8,128)S(1)}, f32[8,256,128]{2,1,0:T(8,128)S(1)}, u32[]{:S(2)}, u32[]{:S(2)}) %collective-permute-start) | collective-permute-done | bytes 1048608 | tf_op jit(solution)/shard_map/ppermute | solution.py:318
  14.0 0.9 add_convert_fusion.2
  15.0 4.2 %all-to-all-start = ((bf16[8,256,128]{2,1,0:T(8,128)(2,1)}), bf16[8,256,128]{2,1,0:T(8,128)(2,1)S(1)}, u32[]{:S(2)}, u32[]{:S(2)}) async-start(bf16[8,256,128]{2,1,0:T(8,128)(2,1)} %add_convert_fusion.2), calls=%async_computation | async-start | bytes 1048576 | tf_op jit(solution)/shard_map/all_to_all | solution.py:322
  19.1 0.8 dynamic_slice.10
  19.9 0.8 dynamic-slice_compare_fusion
  20.7 0.8 convert_rsqrt_fusion
  21.4 7.4 %all-to-all-done = bf16[8,256,128]{2,1,0:T(8,128)(2,1)S(1)} async-done(((bf16[8,256,128]{2,1,0:T(8,128)(2,1)}), bf16[8,256,128]{2,1,0:T(8,128)(2,1)S(1)}, u32[]{:S(2)}, u32[]{:S(2)}) %all-to-all-start) | async-done | bytes 524320 | tf_op jit(solution)/shard_map/all_to_all | solution.py:322
  28.9 0.1 convert_reduce_fusion
  28.9 0.2 select_convert_fusion.1
  29.1 0.1 broadcast_in_dim.42
  29.2 13.4 %all_to_all.15.mine = bf16[8,256,128]{2,1,0:T(8,128)(2,1)S(1)} all-to-all(bf16[8,256,128]{2,1,0:T(8,128)(2,1)S(1)} %broadcast_in_dim.42), channel_id=1, replica_groups=mesh['zlo'=2,'y'=4,'core'=2,'zhi'=4,'x'=4] {'zlo','y'}, dimensions={0} | all-to-all | bytes 1048576 | tf_op jit(solution)/shard_map/all_to_all | solution.py:331
  42.6 1.9 %collective-permute-done.1.partner = bf16[8,256,128]{2,1,0:T(8,128)(2,1)S(1)} collective-permute-done((bf16[8,256,128]{2,1,0:T(8,128)(2,1)S(1)}, bf16[8,256,128]{2,1,0:T(8,128)(2,1)S(1)}, u32[]{:S(2)}, u32[]{:S(2)}) %collective-permute-start.1) | collective-permute-done | bytes 524320 | tf_op jit(solution)/shard_map/ppermute | solution.py:318
  44.5 5.3 %page_partials.3 = (bf16[4,656,128]{2,1,0:T(8,128)(2,1)}, bf16[4,656,128]{2,1,0:T(8,128)(2,1)}) custom-call(s32[48]{0:T(128)S(1)} %concatenate.3.table, bf16[22,512,512]{2,1,0:T(8,128)(2,1)} %bitcast.17, bf16[8,256,128]{2,1,0:T(8,128)(2,1)S(1)} %all_to_all.15.mine, bf16[8,256,128]{2,1,0:T(8,128)(2,1)S(1)} %collective-permute-done.1.partner), custom_call_target="tpu_custom_call" | custom-call | flops 369098752 | bytes 2883584 | tf_op jit(solution)/shard_map/page_partials/pallas_call | solution.py:222
  49.9 0.1 collective-permute-start.3
  50.0 3.2 %collective-permute-start.2 = (bf16[4,656,128]{2,1,0:T(8,128)(2,1)}, bf16[4,656,128]{2,1,0:T(8,128)(2,1)}, u32[]{:S(2)}, u32[]{:S(2)}) collective-permute-start(bf16[4,656,128]{2,1,0:T(8,128)(2,1)} %get-tuple-element.34), channel_id=1, source_target_pairs={{0,1},{1,2},{2,3},{3,0},{4,5},{5,6},{6,7},{7,4},{8,9},{9,10},{10,1... | collective-permute-start | bytes 2015240 | tf_op jit(solution)/shard_map/ppermute | solution.py:248
  53.2 9.6 %page_partials.4 = (bf16[4,656,128]{2,1,0:T(8,128)(2,1)S(1)}, bf16[4,656,128]{2,1,0:T(8,128)(2,1)S(1)}, bf16[4,656,128]{2,1,0:T(8,128)(2,1)S(1)}, bf16[4,656,128...) custom-call(s32[48]{0:T(128)S(1)} %concatenate.3.table, bf16[22,512,512]{2,1,0:T(8,128)(2,1)} %bitcast.18, ...), custom_call_target="tpu_custom_call" | custom-call | flops 1107296256 | bytes 8650752 | tf_op jit(solution)/shard_map/page_partials/pallas_call | solution.py:222
  62.8 0.8 copy-done
  63.7 4.2 %all-to-all-start.2 = ((bf16[4,4,224,128]{3,2,1,0:T(8,128)(2,1)}), bf16[4,4,224,128]{3,2,1,0:T(8,128)(2,1)}, u32[]{:S(2)}, u32[]{:S(2)}) async-start(bf16[4,4,224,128]{3,2,1,0:T(8,128)(2,1)} %get-tuple-element.44), calls=%async_computation.2 | async-start | bytes 1835008 | tf_op jit(solution)/shard_map/all_to_all | solution.py:347
  67.9 0.1 collective-permute-start.12
  68.0 2.0 %collective-permute-start.7 = (bf16[4,656,128]{2,1,0:T(8,128)(2,1)S(1)}, bf16[4,656,128]{2,1,0:T(8,128)(2,1)S(1)}, u32[]{:S(2)}, u32[]{:S(2)}) collective-permute-start(bf16[4,656,128]{2,1,0:T(8,128)(2,1)S(1)} %get-tuple-element.46), channel_id=1, source_target_pairs={{0,3},{1,0},{2,1},{3,2},{4,7},{5,4},{6,5},{7,6},{8,11},{9,8},{10,9... | collective-permute-start | bytes 2015240 | tf_op jit(solution)/shard_map/ppermute | solution.py:248
  70.0 1.3 add_convert_fusion
  71.3 0.0 copy-start.2
  71.3 1.3 add_convert_fusion.1
  72.6 0.1 collective-permute-start.13
  72.7 3.2 %collective-permute-start.8 = (bf16[4,656,128]{2,1,0:T(8,128)(2,1)S(1)}, bf16[4,656,128]{2,1,0:T(8,128)(2,1)S(1)}, u32[]{:S(2)}, u32[]{:S(2)}) collective-permute-start(bf16[4,656,128]{2,1,0:T(8,128)(2,1)S(1)} %add_convert_fusion.1), channel_id=1, source_target_pairs={{0,1},{1,2},{2,3},{3,0},{4,5},{5,6},{6,7},{7,4},{8,9},{9,10},{10,1... | collective-permute-start | bytes 2015240 | tf_op jit(solution)/shard_map/ppermute | solution.py:248
  75.9 1.1 select_convert_fusion.base
  77.0 4.1 %page_partials.5 = (bf16[4,656,128]{2,1,0:T(8,128)(2,1)S(1)}, bf16[4,656,128]{2,1,0:T(8,128)(2,1)S(1)}) custom-call(s32[48]{0:T(128)S(1)} %concatenate.3.table, bf16[22,512,512]{2,1,0:T(8,128)(2,1)} %bitcast.19, bf16[8,256,128]{2,1,0:T(8,128)(2,1)S(1)} %all_to_all.15.mine, bf16[8,256,128]{2,1,0:T(8,128)(2,1)S(1)} %collective-permute-done.1.partner), custom_call_target="tpu_custom_call" | custom-call | flops 369098752 | bytes 2883584 | tf_op jit(solution)/shard_map/page_partials/pallas_call | solution.py:222
  81.2 0.3 broadcast_in_dim.40.scale
  81.4 3.4 %collective-permute-done.12.b = bf16[4,656,128]{2,1,0:T(8,128)(2,1)S(1)} collective-permute-done((bf16[4,656,128]{2,1,0:T(8,128)(2,1)}, bf16[4,656,128]{2,1,0:T(8,128)(2,1)S(1)}, u32[]{:S(2)}, u32[]{:S(2)}) %collective-permute-start.12) | collective-permute-done | bytes 671776 | tf_op jit(solution)/shard_map/ppermute | solution.py:248
  84.9 15.6 %collective-permute-done.13.c = bf16[4,656,128]{2,1,0:T(8,128)(2,1)S(1)} collective-permute-done((bf16[4,656,128]{2,1,0:T(8,128)(2,1)S(1)}, bf16[4,656,128]{2,1,0:T(8,128)(2,1)S(1)}, u32[]{:S(2)}, u32[]{:S(2)}) %collective-permute-start.13) | collective-permute-done | bytes 671776 | tf_op jit(solution)/shard_map/ppermute | solution.py:248
  100.5 0.2 split_sums.3
  100.7 0.1 collective-permute-start.15
  100.8 4.1 %collective-permute-start.14 = (bf16[656,128]{1,0:T(8,128)(2,1)S(1)}, bf16[656,128]{1,0:T(8,128)(2,1)S(1)}, u32[]{:S(2)}, u32[]{:S(2)}) collective-permute-start(bf16[656,128]{1,0:T(8,128)(2,1)S(1)} %get-tuple-element.56), channel_id=1, source_target_pairs={{0,4},{4,8},{8,12},{12,0},{1,5},{5,9},{9,13},{13,1},{2,6},{6,10},{... | collective-permute-start | bytes 503816 | tf_op jit(solution)/shard_map/ppermute | solution.py:248
  104.9 0.2 split_sums.2
  105.2 2.0 %collective-permute-start.10 = (bf16[656,128]{1,0:T(8,128)(2,1)S(1)}, bf16[656,128]{1,0:T(8,128)(2,1)S(1)}, u32[]{:S(2)}, u32[]{:S(2)}) collective-permute-start(bf16[656,128]{1,0:T(8,128)(2,1)S(1)} %get-tuple-element.50), channel_id=1, source_target_pairs={{0,4},{4,8},{8,12},{12,0},{1,5},{5,9},{9,13},{13,1},{2,6},{6,10},{... | collective-permute-start | bytes 503816 | tf_op jit(solution)/shard_map/ppermute | solution.py:248
  107.2 1.0 collective-permute-start.9
  108.2 1.4 %add_convert_fusion.3 = bf16[1,4,224,128]{3,2,1,0:T(8,128)(2,1)S(1)} fusion(bf16[4,4,224,128]{3,2,1,0:T(8,128)(2,1)} %all-to-all-done.2), kind=kLoop, calls=%fused_computation.7 | loop fusion | flops 917504 | bytes 1146880 | tf_op jit(solution)/shard_map/convert
  109.6 0.1 collective-permute-start.4
  109.7 0.5 collective-permute-done.15
  110.2 0.5 collective-permute-start.16
  110.7 9.4 %collective-permute-done.10 = bf16[656,128]{1,0:T(8,128)(2,1)S(1)} collective-permute-done((bf16[656,128]{1,0:T(8,128)(2,1)S(1)}, bf16[656,128]{1,0:T(8,128)(2,1)S(1)}, u32[]{:S(2)}, u32[]{:S(2)}) %collective-permute-start.10) | collective-permute-done | bytes 167968 | tf_op jit(solution)/shard_map/ppermute | solution.py:248
  120.2 4.7 %collective-permute-start.11 = (bf16[656,128]{1,0:T(8,128)(2,1)S(1)}, bf16[656,128]{1,0:T(8,128)(2,1)S(1)}, u32[]{:S(2)}, u32[]{:S(2)}) collective-permute-start(bf16[656,128]{1,0:T(8,128)(2,1)S(1)} %add_convert_fusion.5), channel_id=1, source_target_pairs={{0,4},{4,8},{8,12},{12,0},{1,5},{5,9},{9,13},{13,1},{2,6},{6,10},{... | collective-permute-start | bytes 503816 | tf_op jit(solution)/shard_map/ppermute | solution.py:248
  124.9 5.4 %collective-permute-done.5.s2 = bf16[224,128]{1,0:T(8,128)(2,1)S(1)} collective-permute-done((bf16[224,128]{1,0:T(8,128)(2,1)S(1)}, bf16[224,128]{1,0:T(8,128)(2,1)S(1)}, u32[]{:S(2)}, u32[]{:S(2)}) %collective-permute-start.5) | collective-permute-done | bytes 57376 | tf_op jit(solution)/shard_map/ppermute | solution.py:248
  130.3 5.7 %collective-permute-done.6.s3 = bf16[224,128]{1,0:T(8,128)(2,1)S(1)} collective-permute-done((bf16[224,128]{1,0:T(8,128)(2,1)S(1)}, bf16[224,128]{1,0:T(8,128)(2,1)S(1)}, u32[]{:S(2)}, u32[]{:S(2)}) %collective-permute-start.6) | collective-permute-done | bytes 57376 | tf_op jit(solution)/shard_map/ppermute | solution.py:248
  136.0 1.0 final_sums.1
  (23 shorter events, 0.2 us)
Async XLA Ops:
  11.3 2.7 %collective-permute-start = (f32[8,256,128]{2,1,0:T(8,128)S(1)}, f32[8,256,128]{2,1,0:T(8,128)S(1)}, u32[]{:S(2)}, u32[]{:S(2)}) collective-permute-start(f32[8,256,128]{2,1,0:T(8,128)S(1)} %get-tuple-element.33), channel_id=1, source_target_pairs={{0,16},{16,0},{1,17},{17,1},{2,18},{18,2},{3,19},{19,3},{4,20},{20... | collective-permute-start | bytes 3145736 | tf_op jit(solution)/shard_map/ppermute | solution.py:318
  15.0 13.9 %all-to-all-start = ((bf16[8,256,128]{2,1,0:T(8,128)(2,1)}), bf16[8,256,128]{2,1,0:T(8,128)(2,1)S(1)}, u32[]{:S(2)}, u32[]{:S(2)}) async-start(bf16[8,256,128]{2,1,0:T(8,128)(2,1)} %add_convert_fusion.2), calls=%async_computation | async-start | bytes 1048576 | tf_op jit(solution)/shard_map/all_to_all | solution.py:322
  42.6 1.9 %collective-permute-start.1 = (bf16[8,256,128]{2,1,0:T(8,128)(2,1)S(1)}, bf16[8,256,128]{2,1,0:T(8,128)(2,1)S(1)}, u32[]{:S(2)}, u32[]{:S(2)}) collective-permute-start(bf16[8,256,128]{2,1,0:T(8,128)(2,1)S(1)} %all_to_all.15.mine), channel_id=1, source_target_pairs={{0,16},{16,0},{1,17},{17,1},{2,18},{18,2},{3,19},{19,3},{4,20},{20... | collective-permute-start | bytes 1572872 | tf_op jit(solution)/shard_map/ppermute | solution.py:318
  49.9 20.1 %collective-permute-start.3 = (bf16[4,656,128]{2,1,0:T(8,128)(2,1)}, bf16[4,656,128]{2,1,0:T(8,128)(2,1)}, u32[]{:S(2)}, u32[]{:S(2)}) collective-permute-start(bf16[4,656,128]{2,1,0:T(8,128)(2,1)} %get-tuple-element.36), channel_id=1, source_target_pairs={{0,3},{1,0},{2,1},{3,2},{4,7},{5,4},{6,5},{7,6},{8,11},{9,8},{10,9... | collective-permute-start | bytes 2015240 | tf_op jit(solution)/shard_map/ppermute | solution.py:248
  50.0 21.3 %collective-permute-start.2 = (bf16[4,656,128]{2,1,0:T(8,128)(2,1)}, bf16[4,656,128]{2,1,0:T(8,128)(2,1)}, u32[]{:S(2)}, u32[]{:S(2)}) collective-permute-start(bf16[4,656,128]{2,1,0:T(8,128)(2,1)} %get-tuple-element.34), channel_id=1, source_target_pairs={{0,1},{1,2},{2,3},{3,0},{4,5},{5,6},{6,7},{7,4},{8,9},{9,10},{10,1... | collective-permute-start | bytes 2015240 | tf_op jit(solution)/shard_map/ppermute | solution.py:248
  62.8 0.8 copy-start
  63.7 44.5 %all-to-all-start.2 = ((bf16[4,4,224,128]{3,2,1,0:T(8,128)(2,1)}), bf16[4,4,224,128]{3,2,1,0:T(8,128)(2,1)}, u32[]{:S(2)}, u32[]{:S(2)}) async-start(bf16[4,4,224,128]{3,2,1,0:T(8,128)(2,1)} %get-tuple-element.44), calls=%async_computation.2 | async-start | bytes 1835008 | tf_op jit(solution)/shard_map/all_to_all | solution.py:347
  67.9 17.0 %collective-permute-start.12 = (bf16[4,656,128]{2,1,0:T(8,128)(2,1)}, bf16[4,656,128]{2,1,0:T(8,128)(2,1)S(1)}, u32[]{:S(2)}, u32[]{:S(2)}) collective-permute-start(bf16[4,656,128]{2,1,0:T(8,128)(2,1)} %copy-done), channel_id=1, source_target_pairs={{0,1},{1,2},{2,3},{3,0},{4,5},{5,6},{6,7},{7,4},{8,9},{9,10},{10,1... | collective-permute-start | bytes 2015240 | tf_op jit(solution)/shard_map/ppermute | solution.py:248
  68.0 36.9 %collective-permute-start.7 = (bf16[4,656,128]{2,1,0:T(8,128)(2,1)S(1)}, bf16[4,656,128]{2,1,0:T(8,128)(2,1)S(1)}, u32[]{:S(2)}, u32[]{:S(2)}) collective-permute-start(bf16[4,656,128]{2,1,0:T(8,128)(2,1)S(1)} %get-tuple-element.46), channel_id=1, source_target_pairs={{0,3},{1,0},{2,1},{3,2},{4,7},{5,4},{6,5},{7,6},{8,11},{9,8},{10,9... | collective-permute-start | bytes 2015240 | tf_op jit(solution)/shard_map/ppermute | solution.py:248
  71.3 4.6 %copy-start.2 = (s32[1536]{0:T(1024)S(1)}, s32[1536]{0:T(1024)}, u32[]{:S(2)}) copy-start(s32[1536]{0:T(1024)} %param.18) | copy-start | bytes 18436
  71.3 4.6 %copy-start.3 = (s32[1536]{0:T(1024)S(1)}, s32[1536]{0:T(1024)}, u32[]{:S(2)}) copy-start(s32[1536]{0:T(1024)} %param.16) | copy-start | bytes 18436
  71.3 4.6 %copy-start.1 = (s32[1536]{0:T(1024)S(1)}, s32[1536]{0:T(1024)}, u32[]{:S(2)}) copy-start(s32[1536]{0:T(1024)} %param.17) | copy-start | bytes 18436
  72.6 27.8 %collective-permute-start.13 = (bf16[4,656,128]{2,1,0:T(8,128)(2,1)S(1)}, bf16[4,656,128]{2,1,0:T(8,128)(2,1)S(1)}, u32[]{:S(2)}, u32[]{:S(2)}) collective-permute-start(bf16[4,656,128]{2,1,0:T(8,128)(2,1)S(1)} %add_convert_fusion), channel_id=1, source_target_pairs={{0,3},{1,0},{2,1},{3,2},{4,7},{5,4},{6,5},{7,6},{8,11},{9,8},{10,9... | collective-permute-start | bytes 2015240 | tf_op jit(solution)/shard_map/ppermute | solution.py:248
  72.7 32.2 %collective-permute-start.8 = (bf16[4,656,128]{2,1,0:T(8,128)(2,1)S(1)}, bf16[4,656,128]{2,1,0:T(8,128)(2,1)S(1)}, u32[]{:S(2)}, u32[]{:S(2)}) collective-permute-start(bf16[4,656,128]{2,1,0:T(8,128)(2,1)S(1)} %add_convert_fusion.1), channel_id=1, source_target_pairs={{0,1},{1,2},{2,3},{3,0},{4,5},{5,6},{6,7},{7,4},{8,9},{9,10},{10,1... | collective-permute-start | bytes 2015240 | tf_op jit(solution)/shard_map/ppermute | solution.py:248
  100.7 9.5 %collective-permute-start.15 = (bf16[656,128]{1,0:T(8,128)(2,1)S(1)}, bf16[656,128]{1,0:T(8,128)(2,1)S(1)}, u32[]{:S(2)}, u32[]{:S(2)}) collective-permute-start(bf16[656,128]{1,0:T(8,128)(2,1)S(1)} %get-tuple-element.57), channel_id=1, source_target_pairs={{0,12},{4,0},{8,4},{12,8},{1,13},{5,1},{9,5},{13,9},{2,14},{6,2},{... | collective-permute-start | bytes 503816 | tf_op jit(solution)/shard_map/ppermute | solution.py:248
  100.8 35.2 %collective-permute-start.14 = (bf16[656,128]{1,0:T(8,128)(2,1)S(1)}, bf16[656,128]{1,0:T(8,128)(2,1)S(1)}, u32[]{:S(2)}, u32[]{:S(2)}) collective-permute-start(bf16[656,128]{1,0:T(8,128)(2,1)S(1)} %get-tuple-element.56), channel_id=1, source_target_pairs={{0,4},{4,8},{8,12},{12,0},{1,5},{5,9},{9,13},{13,1},{2,6},{6,10},{... | collective-permute-start | bytes 503816 | tf_op jit(solution)/shard_map/ppermute | solution.py:248
  105.2 15.0 %collective-permute-start.10 = (bf16[656,128]{1,0:T(8,128)(2,1)S(1)}, bf16[656,128]{1,0:T(8,128)(2,1)S(1)}, u32[]{:S(2)}, u32[]{:S(2)}) collective-permute-start(bf16[656,128]{1,0:T(8,128)(2,1)S(1)} %get-tuple-element.50), channel_id=1, source_target_pairs={{0,4},{4,8},{8,12},{12,0},{1,5},{5,9},{9,13},{13,1},{2,6},{6,10},{... | collective-permute-start | bytes 503816 | tf_op jit(solution)/shard_map/ppermute | solution.py:248
  107.2 28.7 %collective-permute-start.9 = (bf16[656,128]{1,0:T(8,128)(2,1)S(1)}, bf16[656,128]{1,0:T(8,128)(2,1)S(1)}, u32[]{:S(2)}, u32[]{:S(2)}) collective-permute-start(bf16[656,128]{1,0:T(8,128)(2,1)S(1)} %get-tuple-element.49), channel_id=1, source_target_pairs={{0,12},{4,0},{8,4},{12,8},{1,13},{5,1},{9,5},{13,9},{2,14},{6,2},{... | collective-permute-start | bytes 503816 | tf_op jit(solution)/shard_map/ppermute | solution.py:248
  109.6 15.3 %collective-permute-start.4 = (bf16[224,128]{1,0:T(8,128)(2,1)S(1)}, bf16[224,128]{1,0:T(8,128)(2,1)S(1)}, u32[]{:S(2)}, u32[]{:S(2)}) collective-permute-start(bf16[224,128]{1,0:T(8,128)(2,1)S(1)} %get-tuple-element.63), channel_id=1, source_target_pairs={{0,1},{1,2},{2,3},{3,0},{4,5},{5,6},{6,7},{7,4},{8,9},{9,10},{10,1... | collective-permute-start | bytes 172040 | tf_op jit(solution)/shard_map/ppermute | solution.py:248
  110.2 25.7 %collective-permute-start.16 = (bf16[656,128]{1,0:T(8,128)(2,1)S(1)}, bf16[656,128]{1,0:T(8,128)(2,1)S(1)}, u32[]{:S(2)}, u32[]{:S(2)}) collective-permute-start(bf16[656,128]{1,0:T(8,128)(2,1)S(1)} %add_convert_fusion.4), channel_id=1, source_target_pairs={{0,12},{4,0},{8,4},{12,8},{1,13},{5,1},{9,5},{13,9},{2,14},{6,2},{... | collective-permute-start | bytes 503816 | tf_op jit(solution)/shard_map/ppermute | solution.py:248
  120.2 15.7 %collective-permute-start.11 = (bf16[656,128]{1,0:T(8,128)(2,1)S(1)}, bf16[656,128]{1,0:T(8,128)(2,1)S(1)}, u32[]{:S(2)}, u32[]{:S(2)}) collective-permute-start(bf16[656,128]{1,0:T(8,128)(2,1)S(1)} %add_convert_fusion.5), channel_id=1, source_target_pairs={{0,4},{4,8},{8,12},{12,0},{1,5},{5,9},{9,13},{13,1},{2,6},{6,10},{... | collective-permute-start | bytes 503816 | tf_op jit(solution)/shard_map/ppermute | solution.py:248
  124.9 5.4 %collective-permute-start.5 = (bf16[224,128]{1,0:T(8,128)(2,1)S(1)}, bf16[224,128]{1,0:T(8,128)(2,1)S(1)}, u32[]{:S(2)}, u32[]{:S(2)}) collective-permute-start(bf16[224,128]{1,0:T(8,128)(2,1)S(1)} %get-tuple-element.62), channel_id=1, source_target_pairs={{0,3},{1,0},{2,1},{3,2},{4,7},{5,4},{6,5},{7,6},{8,11},{9,8},{10,9... | collective-permute-start | bytes 172040 | tf_op jit(solution)/shard_map/ppermute | solution.py:248
  130.3 5.7 %collective-permute-start.6 = (bf16[224,128]{1,0:T(8,128)(2,1)S(1)}, bf16[224,128]{1,0:T(8,128)(2,1)S(1)}, u32[]{:S(2)}, u32[]{:S(2)}) collective-permute-start(bf16[224,128]{1,0:T(8,128)(2,1)S(1)} %get-tuple-element.61), channel_id=1, source_target_pairs={{0,2},{1,3},{2,0},{3,1},{4,6},{5,7},{6,4},{7,5},{8,10},{9,11},{10,... | collective-permute-start | bytes 172040 | tf_op jit(solution)/shard_map/ppermute | solution.py:248
